TPU v7x, 32 devices: a whole 2x2x4 slice. The times are simulated.
32 devices in a mesh: tensor: 4 (over z), dp: 4 (over y, core), ctx: 2 (over x).
Axes of the slice: x: 2, y: 2, z: 4, core: 2. Of those that a mesh axis runs over, the one named last changes fastest.
Arguments:
- block_input: bfloat16 [4, 2, 1024, 768], P('dp', 'ctx', 'tensor'), may hold values from -6 to 6
- seq_lengths: int32 [4, 16], P('dp'), may hold values from 0 to 2048, as said below
- project_weight: bfloat16 [2, 768, 2304], P(None, ('dp', 'ctx'), 'tensor'), may hold values from -0.21875 to 0.21875
- project_bias: bfloat16 [2, 2304], P(None, ('tensor', 'dp', 'ctx')), may hold values from -3 to 3
- dense_weight: bfloat16 [2, 768, 768], P(None, ('tensor', 'dp', 'ctx')), may hold values from -0.75 to 0.75
- up_weight: bfloat16 [2, 768, 3072], P(None, ('dp', 'ctx'), 'tensor'), may hold values from -0.21875 to 0.21875
- up_bias: bfloat16 [2, 3072], P(None, ('tensor', 'dp', 'ctx')), may hold values from -3 to 3
- down_weight: bfloat16 [2, 3072, 768], P(None, ('tensor', 'dp', 'ctx')), may hold values from -0.109375 to 0.109375
- norm_gains: bfloat16 [2, 768, 2], replicated, may hold values from 0.5 to 1.5
- shift_vectors: bfloat16 [2, 768, 4], replicated, may hold values from -2 to 2
- cotangent: float32 [4, 2, 1024, 768], P('dp', 'ctx', 'tensor'), may hold values from -6 to 6
Outputs:
- block_output: float32 [4, 2, 1024, 768], P('dp', 'ctx', 'tensor')
- input_grad: float32 [4, 2, 1024, 768], P('dp', 'ctx', 'tensor')
- project_weight_grad: float32 [2, 768, 2304], P(None, ('dp', 'ctx'), 'tensor')
- project_bias_grad: float32 [2, 2304], P(None, ('tensor', 'dp', 'ctx'))
- dense_weight_grad: float32 [2, 768, 768], P(None, ('tensor', 'dp', 'ctx'))
- up_weight_grad: float32 [2, 768, 3072], P(None, ('dp', 'ctx'), 'tensor')
- up_bias_grad: float32 [2, 3072], P(None, ('tensor', 'dp', 'ctx'))
- down_weight_grad: float32 [2, 3072, 768], P(None, ('tensor', 'dp', 'ctx'))
- norm_gains_grad: float32 [2, 768, 2], P(None, ('tensor', 'dp', 'ctx'))
- shift_vectors_grad: float32 [2, 768, 4], P(None, ('tensor', 'dp', 'ctx'))
Inputs may be any that keep to these rules, and one draw needn't show every extreme that they name: `seq_lengths`: each row's entries sum to 2048; its nonzero entries come first, and each of them but the last is 128 or more; a row's slots hold its sequences one after another in this order.
All inputs are finite; a program needn't handle non-finite values.
Results may differ from a plain program's by a relative error of at most 0.018.
Values may be sent and summed in bfloat16 or wider, within the bound.
No kernel may reach another device: no remote copies, remote signals or barrier semaphores. Data moves between devices by JAX's collectives and lax.ppermute only.
A program may use at most 128 MiB of HBM per device.

v0:
```python
from functools import partial

import jax
import jax.numpy as jnp
from jax import lax
from jax.sharding import PartitionSpec as P

HEAD_DIM = 64
ROTARY = 16
LAYERS = 2


EPSILON = 1e-05
MASKED = -1e30


def row_tables(lengths, first_slot, count):
    ends = jnp.cumsum(lengths, axis=1)
    slots = first_slot + jnp.arange(count, dtype=jnp.int32)
    passed = (ends[:, None, :] <= slots[None, :, None]).astype(jnp.int32)
    segment = jnp.sum(passed, axis=2)
    begin = jnp.sum(passed * lengths[:, None, :], axis=2)
    return (segment, slots[None, :] - begin)


def rotary_tables(position):
    frequency = 1.0 / 10000.0 ** (jnp.arange(0, ROTARY, 2, dtype=jnp.float32) / ROTARY)
    angle = position.astype(jnp.float32)[..., None] * frequency
    angle = jnp.concatenate([angle, angle], axis=-1)[..., None, :]
    return (jnp.cos(angle), jnp.sin(angle))


def rotate(vectors, cosine, sine):
    head = vectors[..., :ROTARY]
    half = ROTARY // 2
    turned = jnp.concatenate([-head[..., half:], head[..., :half]], axis=-1)
    return jnp.concatenate([head * cosine + turned * sine, vectors[..., ROTARY:]], axis=-1)


def unrotate(grads, cosine, sine):
    head = grads[..., :ROTARY]
    half = ROTARY // 2
    scaled = head * sine
    back = jnp.concatenate([scaled[..., half:], -scaled[..., :half]], axis=-1)
    return jnp.concatenate([head * cosine + back, grads[..., ROTARY:]], axis=-1)


def normalize(values):
    centre = values - jnp.mean(values, axis=-1, keepdims=True)
    inverse = lax.rsqrt(jnp.mean(centre * centre, axis=-1, keepdims=True) + EPSILON)
    return (centre * inverse, inverse)


def block_scores(query, pairs, segment_row, segment_mine, first_query, index, block_len):
    size = query.shape[-1]
    start = index * block_len
    block = lax.dynamic_slice_in_dim(pairs, start, block_len, 1)
    keys = block[..., :size]
    values = block[..., size:]
    scores = jnp.einsum(
        "rqhd,rkhd->rhqk", query, keys, preferred_element_type=jnp.float32
    ) * HEAD_DIM ** (-0.5)
    key_segment = lax.dynamic_slice_in_dim(segment_row, start, block_len, 1)
    query_slots = first_query + jnp.arange(query.shape[1], dtype=jnp.int32)
    key_slots = start + jnp.arange(block_len, dtype=jnp.int32)
    allowed = (segment_mine[:, :, None] == key_segment[:, None, :]) & (
        key_slots[None, None, :] <= query_slots[None, :, None]
    )
    return (jnp.where(allowed[:, None], scores, MASKED), keys, values)


def attend(query, pairs, segment_row, segment_mine, place, block_len):
    rows, count, heads, size = query.shape
    first_query = place * block_len
    turns = place + 1

    def scores_at(index):
        return block_scores(query, pairs, segment_row, segment_mine, first_query, index, block_len)

    def add_stats(index, carry):
        top, total = carry
        scores = scores_at(index)[0]
        newer = jnp.maximum(top, jnp.max(scores, axis=-1))
        total = total * jnp.exp(top - newer) + jnp.sum(jnp.exp(scores - newer[..., None]), axis=-1)
        return (newer, total)

    start_stats = (
        jnp.full((rows, heads, count), MASKED, jnp.float32),
        jnp.zeros((rows, heads, count), jnp.float32),
    )
    top, total = lax.fori_loop(0, turns, add_stats, start_stats)
    log_total = top + jnp.log(total)

    def add_mixed(index, mixed):
        scores, _, values = scores_at(index)
        weights = jnp.exp(scores - log_total[..., None]).astype(jnp.bfloat16)
        return mixed + jnp.einsum(
            "rhqk,rkhd->rqhd", weights, values, preferred_element_type=jnp.float32
        )

    mixed = lax.fori_loop(0, turns, add_mixed, jnp.zeros((rows, count, heads, size), jnp.float32))
    return (mixed, log_total)


def attend_back(query, pairs, segment_row, segment_mine, place, block_len, log_total, grad_mixed):
    rows, count, heads, size = query.shape
    first_query = place * block_len
    turns = place + 1
    scale = HEAD_DIM ** (-0.5)

    def scores_at(index):
        return block_scores(query, pairs, segment_row, segment_mine, first_query, index, block_len)

    def add_delta(index, delta):
        scores, _, values = scores_at(index)
        probability = jnp.exp(scores - log_total[..., None])
        grad_probs = jnp.einsum(
            "rqhd,rkhd->rhqk", grad_mixed, values, preferred_element_type=jnp.float32
        )
        return delta + jnp.sum(probability * grad_probs, axis=-1)

    delta = lax.fori_loop(0, turns, add_delta, jnp.zeros((rows, heads, count), jnp.float32))

    def add_grads(index, carry):
        grad_query, grad_pairs = carry
        scores, keys, values = scores_at(index)
        probability = jnp.exp(scores - log_total[..., None])
        grad_probs = jnp.einsum(
            "rqhd,rkhd->rhqk", grad_mixed, values, preferred_element_type=jnp.float32
        )
        grad_scores = (probability * (grad_probs - delta[..., None])).astype(jnp.bfloat16)
        grad_query = (
            grad_query
            + jnp.einsum("rhqk,rkhd->rqhd", grad_scores, keys, preferred_element_type=jnp.float32)
            * scale
        )
        grad_keys = (
            jnp.einsum("rhqk,rqhd->rkhd", grad_scores, query, preferred_element_type=jnp.float32)
            * scale
        )
        grad_values = jnp.einsum(
            "rhqk,rqhd->rkhd",
            probability.astype(jnp.bfloat16),
            grad_mixed,
            preferred_element_type=jnp.float32,
        )
        grad_pairs = lax.dynamic_update_slice_in_dim(
            grad_pairs, jnp.concatenate([grad_keys, grad_values], axis=-1), index * block_len, 1
        )
        return (grad_query, grad_pairs)

    empty_pairs = jnp.zeros(pairs.shape, jnp.float32)
    grad_query, grad_pairs = lax.fori_loop(
        0, turns, add_grads, (jnp.zeros(query.shape, jnp.float32), empty_pairs)
    )
    return (grad_query, grad_pairs, delta)


def norm_backward(summed, unit_local, inverse_local):
    mean_s = jnp.mean(summed, axis=-1, keepdims=True)
    mean_su = jnp.mean(summed * unit_local, axis=-1, keepdims=True)
    return inverse_local * (summed - mean_s - unit_local * mean_su)


def shards(
    block_input,
    seq_lengths,
    project_weight,
    project_bias,
    dense_weight,
    up_weight,
    up_bias,
    down_weight,
    norm_gains,
    shift_vectors,
    cotangent,
):
    rows, _, own_count, width = block_input.shape
    places = lax.axis_size("ctx")
    place = lax.axis_index("ctx")
    block_len = own_count * lax.axis_size("tensor")
    row_len = block_len * places
    token_start = lax.axis_index("tensor") * own_count
    segment_row, _ = row_tables(seq_lengths, 0, row_len)
    segment_mine, position = row_tables(seq_lengths, place * block_len, block_len)
    cosine, sine = rotary_tables(position)
    gains = norm_gains.astype(jnp.float32)
    shifts = shift_vectors.astype(jnp.float32)
    residual = block_input[:, 0].astype(jnp.float32)
    stored = []
    for layer in range(LAYERS):
        fetched = (
            lax.all_gather(project_weight[layer], ("dp", "ctx"), axis=0, tiled=True),
            lax.all_gather(up_weight[layer], ("dp", "ctx"), axis=0, tiled=True),
            lax.all_gather(dense_weight[layer], ("dp", "ctx"), axis=0, tiled=True),
            lax.all_gather(down_weight[layer], ("dp", "ctx"), axis=0, tiled=True),
            lax.all_gather(project_bias[layer], ("dp", "ctx"), axis=0, tiled=True),
            lax.all_gather(up_bias[layer], ("dp", "ctx"), axis=0, tiled=True),
        )
        mix_w, up_w, dense_w, down_w, mix_b, up_b = fetched
        whole = lax.all_gather(residual.astype(jnp.bfloat16), "tensor", axis=1, tiled=True).astype(
            jnp.float32
        )
        unit, inverse = normalize(whole)
        first = (unit * gains[layer, :, 0] + shifts[layer, :, 0]).astype(jnp.bfloat16)
        second = (unit * gains[layer, :, 1] + shifts[layer, :, 1]).astype(jnp.bfloat16)
        projected = jnp.einsum(
            "rcd,de->rce", first, mix_w, preferred_element_type=jnp.float32
        ) + mix_b.astype(jnp.float32)
        projected = projected.reshape(rows, block_len, -1, 3, HEAD_DIM)
        query = rotate(projected[:, :, :, 0], cosine, sine).astype(jnp.bfloat16)
        keys = rotate(projected[:, :, :, 1], cosine, sine).astype(jnp.bfloat16)
        values = projected[:, :, :, 2].astype(jnp.bfloat16)
        pairs = lax.all_gather(jnp.concatenate([keys, values], axis=-1), "ctx", axis=1, tiled=True)
        mixed, log_total = attend(query, pairs, segment_row, segment_mine, place, block_len)
        mixed = mixed.astype(jnp.bfloat16).reshape(rows, block_len, -1)
        hidden = jnp.einsum(
            "rcd,df->rcf", second, up_w, preferred_element_type=jnp.float32
        ) + up_b.astype(jnp.float32)
        active = jax.nn.gelu(hidden, approximate=False).astype(jnp.bfloat16)
        branch = jnp.einsum(
            "rci,id->rcd", mixed, dense_w, preferred_element_type=jnp.float32
        ) + jnp.einsum("rcf,fd->rcd", active, down_w, preferred_element_type=jnp.float32)
        share = lax.psum_scatter(
            branch.astype(jnp.bfloat16), "tensor", scatter_dimension=1, tiled=True
        ).astype(jnp.float32)
        residual = residual + share + shifts[layer, :, 2] + shifts[layer, :, 3]
        kept_weights = None
        stored.append(
            (
                kept_weights,
                unit,
                inverse,
                first,
                second,
                query,
                pairs,
                log_total,
                mixed,
                hidden,
                active,
            )
        )
    grad = cotangent[:, 0]
    outputs = []
    small_outputs = []
    for layer in reversed(range(LAYERS)):
        (
            kept_weights,
            unit,
            inverse,
            first,
            second,
            query,
            pairs,
            log_total,
            mixed,
            hidden,
            active,
        ) = stored[layer]
        fetched = (
            lax.all_gather(project_weight[layer], ("dp", "ctx"), axis=0, tiled=True),
            lax.all_gather(up_weight[layer], ("dp", "ctx"), axis=0, tiled=True),
            lax.all_gather(dense_weight[layer], ("dp", "ctx"), axis=0, tiled=True),
            lax.all_gather(down_weight[layer], ("dp", "ctx"), axis=0, tiled=True),
            lax.all_gather(project_bias[layer], ("dp", "ctx"), axis=0, tiled=True),
            lax.all_gather(up_bias[layer], ("dp", "ctx"), axis=0, tiled=True),
        )
        mix_w, up_w, dense_w, down_w, mix_b, up_b = fetched
        grad_branch = lax.all_gather(grad.astype(jnp.bfloat16), "tensor", axis=1, tiled=True)
        grad_dense_w = jnp.einsum(
            "rci,rcd->id", mixed, grad_branch, preferred_element_type=jnp.float32
        )
        grad_down_w = jnp.einsum(
            "rcf,rcd->fd", active, grad_branch, preferred_element_type=jnp.float32
        )
        grad_mixed = jnp.einsum(
            "rcd,id->rci", grad_branch, dense_w, preferred_element_type=jnp.float32
        ).astype(jnp.bfloat16)
        grad_mixed = grad_mixed.reshape(rows, block_len, -1, HEAD_DIM)
        grad_active = jnp.einsum(
            "rcd,fd->rcf", grad_branch, down_w, preferred_element_type=jnp.float32
        )
        _, gelu_back = jax.vjp(partial(jax.nn.gelu, approximate=False), hidden)
        grad_hidden = gelu_back(grad_active)[0].astype(jnp.bfloat16)
        grad_up_w = jnp.einsum(
            "rcd,rcf->df", second, grad_hidden, preferred_element_type=jnp.float32
        )
        grad_up_b = jnp.sum(grad_hidden.astype(jnp.float32), axis=(0, 1))
        grad_second = jnp.einsum(
            "rcf,df->rcd", grad_hidden, up_w, preferred_element_type=jnp.float32
        )
        grad_query, grad_pairs, _ = attend_back(
            query, pairs, segment_row, segment_mine, place, block_len, log_total, grad_mixed
        )
        grad_pairs = lax.psum_scatter(
            grad_pairs.astype(jnp.bfloat16), "ctx", scatter_dimension=1, tiled=True
        ).astype(jnp.float32)
        grad_query_raw = unrotate(grad_query, cosine, sine)
        grad_keys_raw = unrotate(grad_pairs[..., :HEAD_DIM], cosine, sine)
        grad_projected = jnp.stack(
            [grad_query_raw, grad_keys_raw, grad_pairs[..., HEAD_DIM:]], axis=3
        )
        grad_projected = grad_projected.reshape(rows, block_len, -1).astype(jnp.bfloat16)
        grad_mix_w = jnp.einsum(
            "rcd,rce->de", first, grad_projected, preferred_element_type=jnp.float32
        )
        grad_mix_b = jnp.sum(grad_projected.astype(jnp.float32), axis=(0, 1))
        grad_first = jnp.einsum(
            "rce,de->rcd", grad_projected, mix_w, preferred_element_type=jnp.float32
        )
        unit_local = lax.dynamic_slice_in_dim(unit, token_start, own_count, 1)
        inverse_local = lax.dynamic_slice_in_dim(inverse, token_start, own_count, 1)
        token_sum = jnp.sum(grad, axis=(0, 1))
        first_share, second_share = (
            lax.psum_scatter(
                grad_first.astype(jnp.bfloat16), "tensor", scatter_dimension=1, tiled=True
            ).astype(jnp.float32),
            lax.psum_scatter(
                grad_second.astype(jnp.bfloat16), "tensor", scatter_dimension=1, tiled=True
            ).astype(jnp.float32),
        )
        scaled_a = first_share * gains[layer, :, 0]
        scaled_b = second_share * gains[layer, :, 1]
        norm_back = norm_backward(scaled_a, unit_local, inverse_local) + norm_backward(
            scaled_b, unit_local, inverse_local
        )
        gain_grad = jnp.stack(
            [
                jnp.sum(first_share * unit_local, axis=(0, 1)),
                jnp.sum(second_share * unit_local, axis=(0, 1)),
            ],
            axis=-1,
        )
        shift_grad = jnp.stack(
            [
                jnp.sum(first_share, axis=(0, 1)),
                jnp.sum(second_share, axis=(0, 1)),
                token_sum,
                token_sum,
            ],
            axis=-1,
        )
        summed = (
            lax.psum_scatter(
                grad_mix_w.astype(jnp.bfloat16), ("dp", "ctx"), scatter_dimension=0, tiled=True
            ).astype(jnp.float32),
            lax.psum_scatter(
                grad_up_w.astype(jnp.bfloat16), ("dp", "ctx"), scatter_dimension=0, tiled=True
            ).astype(jnp.float32),
            lax.psum_scatter(
                grad_dense_w.astype(jnp.bfloat16), ("dp", "ctx"), scatter_dimension=0, tiled=True
            ).astype(jnp.float32),
            lax.psum_scatter(
                grad_down_w.astype(jnp.bfloat16), ("dp", "ctx"), scatter_dimension=0, tiled=True
            ).astype(jnp.float32),
            lax.psum_scatter(
                grad_mix_b.astype(jnp.bfloat16), ("dp", "ctx"), scatter_dimension=0, tiled=True
            ).astype(jnp.float32),
            lax.psum_scatter(
                grad_up_b.astype(jnp.bfloat16), ("dp", "ctx"), scatter_dimension=0, tiled=True
            ).astype(jnp.float32),
        )
        small = (
            lax.psum_scatter(gain_grad, ("tensor", "dp", "ctx"), scatter_dimension=0, tiled=True),
            lax.psum_scatter(shift_grad, ("tensor", "dp", "ctx"), scatter_dimension=0, tiled=True),
        )
        outputs.append(summed)
        small_outputs.append(small)
        grad = grad + norm_back
    outputs = outputs[::-1]
    small_outputs = small_outputs[::-1]
    stacked = [jnp.stack([item[number] for item in outputs]) for number in range(6)]
    gains_out = jnp.stack([item[0] for item in small_outputs])
    shifts_out = jnp.stack([item[1] for item in small_outputs])
    return (
        residual[:, None],
        grad[:, None],
        stacked[0],
        stacked[4],
        stacked[2],
        stacked[1],
        stacked[5],
        stacked[3],
        gains_out,
        shifts_out,
    )


def solution(mesh):
    in_specs = (
        P("dp", "ctx", "tensor", None),
        P("dp", None),
        P(None, ("dp", "ctx"), "tensor"),
        P(None, ("tensor", "dp", "ctx")),
        P(None, ("tensor", "dp", "ctx"), None),
        P(None, ("dp", "ctx"), "tensor"),
        P(None, ("tensor", "dp", "ctx")),
        P(None, ("tensor", "dp", "ctx"), None),
        P(),
        P(),
        P("dp", "ctx", "tensor", None),
    )
    out_specs = (
        P("dp", "ctx", "tensor", None),
        P("dp", "ctx", "tensor", None),
        P(None, ("dp", "ctx"), "tensor"),
        P(None, ("tensor", "dp", "ctx")),
        P(None, ("tensor", "dp", "ctx"), None),
        P(None, ("dp", "ctx"), "tensor"),
        P(None, ("tensor", "dp", "ctx")),
        P(None, ("tensor", "dp", "ctx"), None),
        P(None, ("tensor", "dp", "ctx"), None),
        P(None, ("tensor", "dp", "ctx"), None),
    )
    return jax.shard_map(shards, mesh=mesh, in_specs=in_specs, out_specs=out_specs, check_vma=False)
```

profile of v0, /device:TPU:0, one launch (start us, length us, event | category | flops | bytes accessed | tf_op | source)
XLA Modules:
  0.0 1150.1 jit_solution(8971154575651536758)
XLA Ops:
  16.5 16.5 %all-reduce.14 = (bf16[768]{0:T(1024)(128)(2,1)S(1)}, bf16[576]{0:T(1024)(128)(2,1)S(1)}, bf16[768]{0:T(1024)(128)(2,1)S(1)}, bf16[576]{0:T(1024)(128)(2,1)}) all-reduce(bf16[768]{0:T(1024)(128)(2,1)S(1)} %dynamic-update-slice.1, bf16[576]{0:T(1024)(128)(2,1)S(1)} %dynamic-update-slice, ...), channel_id=7, replica_groups=mesh['tensor'=4,'dp'=4,'ctx'=2] {'dp','ctx'}, use_global_device_ids=true, to_apply=%add.1 | all-reduce | flops 2688 | bytes 10752
  37.3 19.2 %all-gather.1 = bf16[1,768,576]{2,1,0:T(8,128)(2,1)S(1)} all-gather(bf16[1,96,576]{2,1,0:T(8,128)(2,1)S(1)} %get-tuple-element.741), channel_id=3, replica_groups=mesh['tensor'=4,'dp'=4,'ctx'=2] {'dp','ctx'}, dimensions={1}, use_global_device_ids=true | all-gather | bytes 995328 | tf_op jit(solution)/shard_map/all_gather | solution.py:193
  57.9 18.6 %all-gather.3 = bf16[1,192,768]{2,1,0:T(8,128)(2,1)} all-gather(bf16[1,24,768]{2,1,0:T(8,128)(2,1)S(1)} %get-tuple-element.755), channel_id=5, replica_groups=mesh['tensor'=4,'dp'=4,'ctx'=2] {'dp','ctx'}, dimensions={1}, use_global_device_ids=true | all-gather | bytes 331776 | tf_op jit(solution)/shard_map/all_gather | solution.py:195
  107.9 24.4 %all-gather.24.cloned.1.call-done = bf16[1,2048,3,128]{1,3,2,0:T(8,128)(2,1)} async-done(((bf16[1,1024,3,128]{1,3,2,0:T(8,128)(2,1)}), bf16[1,2048,3,128]{1,3,2,0:T(8,128)(2,1)}) %all-gather.24.cloned.1.call-update) | async-done | bytes 1572880 | tf_op jit(solution)/shard_map/all_gather | solution.py:214
  153.1 51.6 %reduce-scatter.21.cloned.1.call-done = bf16[1,256,768]{2,1,0:T(8,128)(2,1)} async-done(((bf16[1,1024,768]{2,1,0:T(8,128)(2,1)}), bf16[1,256,768]{2,1,0:T(8,128)(2,1)}) %reduce-scatter.21.cloned.1.call-update) | async-done | bytes 393232 | tf_op jit(solution)/shard_map/reduce_scatter | solution.py:224
  208.2 19.4 %all-gather.7 = bf16[1,768,576]{2,1,0:T(8,128)(2,1)S(1)} all-gather(bf16[1,96,576]{2,1,0:T(8,128)(2,1)S(1)} %copy-done.38), channel_id=9, replica_groups=mesh['tensor'=4,'dp'=4,'ctx'=2] {'dp','ctx'}, dimensions={1}, use_global_device_ids=true | all-gather | bytes 995328 | tf_op jit(solution)/shard_map/all_gather | solution.py:193
  227.6 15.3 %all-gather.26.cloned.1.call-done = bf16[1,1024,768]{2,1,0:T(8,128)(2,1)} async-done(((bf16[1,256,768]{2,1,0:T(8,128)(2,1)}), bf16[1,1024,768]{2,1,0:T(8,128)(2,1)}) %all-gather.26.cloned.1.call-update) | async-done | bytes 1572880 | tf_op jit(solution)/shard_map/all_gather | solution.py:201
  252.2 17.3 %all-gather.9 = bf16[1,192,768]{2,1,0:T(8,128)(2,1)S(1)} all-gather(bf16[1,24,768]{2,1,0:T(8,128)(2,1)S(1)} %copy-done.39), channel_id=11, replica_groups=mesh['tensor'=4,'dp'=4,'ctx'=2] {'dp','ctx'}, dimensions={1}, use_global_device_ids=true | all-gather | bytes 331776 | tf_op jit(solution)/shard_map/all_gather | solution.py:195
  283.9 25.3 %all-gather.28.cloned.1.call-done = bf16[1,2048,3,128]{1,3,2,0:T(8,128)(2,1)} async-done(((bf16[1,1024,3,128]{1,3,2,0:T(8,128)(2,1)}), bf16[1,2048,3,128]{1,3,2,0:T(8,128)(2,1)}) %all-gather.28.cloned.1.call-update) | async-done | bytes 1572880 | tf_op jit(solution)/shard_map/all_gather | solution.py:214
  318.6 16.1 %while.92 = (s32[]{:T(128)}, f32[1,3,1024]{2,1,0:T(4,128)S(1)}, s32[]{:T(128)}, s32[1,1024]{1,0:T(1,128)S(1)}, s32[1,2048]{1,0:T(1,128)S(1)}, /*index=5*/s32[]{:...) while((s32[]{:T(128)}, f32[1,3,1024]{2,1,0:T(4,128)S(1)}, ...), condition=%wide.region_24.25_spmd, body=%wide.region_22.24_spmd.sunk | while | flops 824182784 | bytes 30503164 | solution.py:122
  336.2 28.4 %while.93 = (s32[]{:T(128)}, f32[1,1024,3,64]{1,3,2,0:T(8,128)S(1)}, bf16[1,2048,3,128]{1,3,2,0:T(8,128)(2,1)}, s32[]{:T(128)}, bf16[1,2048,3,128]{1,3,2,0:T(8,1...) while((s32[]{:T(128)}, ...), condition=%wide.region_26.27_spmd, body=%wide.region_25.26_spmd.sunk | while | flops 2050230272 | bytes 68096272 | solution.py:153
  364.8 11.9 %multiply_convert_fusion = (bf16[1024,768]{1,0:T(8,128)(2,1)}, f32[1024,768]{1,0:T(8,128)}, f32[1024,768]{1,0:T(8,128)}) fusion(f32[768]{0:T(1024)S(1)} %copy-done.82, bf16[1,768,768]{2,1,0:T(8,128)(2,1)} %all-gather.40.cloned.1.call-done, f32[768]{0:T(1024)S(1)} %copy-done.78, f32[768]{0:T(1024)S(1)} %copy-done.52, f32[1024]{0:T(1024)S(1)} %copy-done.64, ...), kind=kOutput, calls=%fused_computation.178 | convolution fusion | flops 1264582656 | bytes 10634240 | tf_op jit(solution)/shard_map/rcd,df->rcf/dot_general | solution.py:217
  386.7 57.1 %reduce-scatter.25.cloned.1.call-done = bf16[1,1024,3,128]{1,3,2,0:T(8,128)(2,1)} async-done(((bf16[1,2048,3,128]{1,3,2,0:T(8,128)(2,1)}), bf16[1,1024,3,128]{1,3,2,0:T(8,128)(2,1)}) %reduce-scatter.25.cloned.1.call-update) | async-done | bytes 786448 | tf_op jit(solution)/shard_map/reduce_scatter | solution.py:296
  452.2 29.2 %reduce-scatter.29.cloned.1.call-done = bf16[1,256,768]{2,1,0:T(8,128)(2,1)} async-done(((bf16[1,1024,768]{2,1,0:T(8,128)(2,1)}), bf16[1,256,768]{2,1,0:T(8,128)(2,1)}) %reduce-scatter.29.cloned.1.call-update) | async-done | bytes 393232 | tf_op jit(solution)/shard_map/reduce_scatter | solution.py:319
  481.3 36.7 %reduce-scatter.27.cloned.1.call-done = bf16[1,256,768]{2,1,0:T(8,128)(2,1)} async-done(((bf16[1,1024,768]{2,1,0:T(8,128)(2,1)}), bf16[1,256,768]{2,1,0:T(8,128)(2,1)}) %reduce-scatter.27.cloned.1.call-update) | async-done | bytes 393232 | tf_op jit(solution)/shard_map/reduce_scatter | solution.py:316
  530.1 30.7 %all-gather.32.cloned.1.call-done = bf16[1,1024,768]{2,1,0:T(8,128)(2,1)} async-done(((bf16[1,256,768]{2,1,0:T(8,128)(2,1)}), bf16[1,1024,768]{2,1,0:T(8,128)(2,1)}) %all-gather.32.cloned.1.call-update) | async-done | bytes 1572880 | tf_op jit(solution)/shard_map/all_gather | solution.py:270
  563.7 14.6 %while.94 = (s32[]{:T(128)}, f32[1,3,1024]{2,1,0:T(4,128)S(1)}, s32[]{:T(128)}, s32[1,1024]{1,0:T(1,128)S(1)}, s32[1,2048]{1,0:T(1,128)S(1)}, /*index=5*/s32[]{:...) while((s32[]{:T(128)}, f32[1,3,1024]{2,1,0:T(4,128)S(1)}, ...), condition=%wide.region_36.37_spmd, body=%wide.region_34.36_spmd.sunk | while | flops 824182784 | bytes 28934368 | solution.py:122
  579.8 28.0 %while.95 = (s32[]{:T(128)}, f32[1,1024,3,64]{1,3,2,0:T(8,128)S(1)}, bf16[1,2048,3,128]{1,3,2,0:T(8,128)(2,1)}, s32[]{:T(128)}, bf16[1,2048,3,128]{1,3,2,0:T(8,1...) while((s32[]{:T(128)}, ...), condition=%wide.region_38.39_spmd, body=%wide.region_37.38_spmd.sunk | while | flops 2050230272 | bytes 68096272 | solution.py:153
  651.7 23.7 %reduce-scatter.31.cloned.1.call-done = bf16[1,1024,3,128]{1,3,2,0:T(8,128)(2,1)} async-done(((bf16[1,2048,3,128]{1,3,2,0:T(8,128)(2,1)}), bf16[1,1024,3,128]{1,3,2,0:T(8,128)(2,1)}) %reduce-scatter.31.cloned.1.call-update) | async-done | bytes 786448 | tf_op jit(solution)/shard_map/reduce_scatter | solution.py:296
  695.4 17.5 %reduce-scatter.23.cloned.1.call-done = bf16[1,256,768]{2,1,0:T(8,128)(2,1)} async-done(((bf16[1,1024,768]{2,1,0:T(8,128)(2,1)}), bf16[1,256,768]{2,1,0:T(8,128)(2,1)}) %reduce-scatter.23.cloned.1.call-update) | async-done | bytes 393232 | tf_op jit(solution)/shard_map/reduce_scatter | solution.py:224
  719.4 29.0 %reduce-scatter.43.cloned.1.call-done = bf16[24,768]{1,0:T(8,128)(2,1)} async-done(((bf16[192,768]{1,0:T(8,128)(2,1)}), bf16[24,768]{1,0:T(8,128)(2,1)}) %reduce-scatter.43.cloned.1.call-update) | async-done | bytes 36880 | tf_op jit(solution)/shard_map/reduce_scatter | solution.py:351
  748.3 36.4 %reduce-scatter.41.cloned.1.call-done = bf16[24,768]{1,0:T(8,128)(2,1)} async-done(((bf16[192,768]{1,0:T(8,128)(2,1)}), bf16[24,768]{1,0:T(8,128)(2,1)}) %reduce-scatter.41.cloned.1.call-update) | async-done | bytes 36880 | tf_op jit(solution)/shard_map/reduce_scatter | solution.py:351
  786.2 38.6 %reduce-scatter.51.cloned.1.call-done = bf16[96,768]{1,0:T(8,128)(2,1)} async-done(((bf16[768,768]{1,0:T(8,128)(2,1)}), bf16[96,768]{1,0:T(8,128)(2,1)}) %reduce-scatter.51.cloned.1.call-update) | async-done | bytes 147472 | tf_op jit(solution)/shard_map/reduce_scatter | solution.py:354
  824.7 40.2 %reduce-scatter.49.cloned.1.call-done = bf16[96,768]{1,0:T(8,128)(2,1)} async-done(((bf16[768,768]{1,0:T(8,128)(2,1)}), bf16[96,768]{1,0:T(8,128)(2,1)}) %reduce-scatter.49.cloned.1.call-update) | async-done | bytes 147472 | tf_op jit(solution)/shard_map/reduce_scatter | solution.py:354
  866.7 38.2 %reduce-scatter.47.cloned.1.call-done = bf16[96,768]{1,0:T(8,128)(2,1)} async-done(((bf16[768,768]{1,0:T(8,128)(2,1)}), bf16[96,768]{1,0:T(8,128)(2,1)}) %reduce-scatter.47.cloned.1.call-update) | async-done | bytes 147472 | tf_op jit(solution)/shard_map/reduce_scatter | solution.py:348
  904.9 40.4 %reduce-scatter.45.cloned.1.call-done = bf16[96,768]{1,0:T(8,128)(2,1)} async-done(((bf16[768,768]{1,0:T(8,128)(2,1)}), bf16[96,768]{1,0:T(8,128)(2,1)}) %reduce-scatter.45.cloned.1.call-update) | async-done | bytes 147472 | tf_op jit(solution)/shard_map/reduce_scatter | solution.py:348
  947.9 14.0 %all-reduce.13 = (bf16[576]{0:T(1024)(128)(2,1)S(1)}, bf16[576]{0:T(1024)(128)(2,1)S(1)}, bf16[768]{0:T(1024)(128)(2,1)S(1)}, bf16[768]{0:T(1024)(128)(2,1)S(1)}) all-reduce(bf16[576]{0:T(1024)(128)(2,1)} %reduce_sum.345, bf16[576]{0:T(1024)(128)(2,1)S(1)} %reduce_sum.343, ...), channel_id=26, replica_groups=mesh['tensor'=4,'dp'=4,'ctx'=2] {'dp','ctx'}, use_global_device_ids=true, to_apply=%region_51.52.clone | all-reduce | flops 2688 | bytes 10752
  963.4 20.9 %reduce-scatter.39.cloned.1.call-done = bf16[96,576]{1,0:T(8,128)(2,1)} async-done(((bf16[768,576]{1,0:T(8,128)(2,1)}), bf16[96,576]{1,0:T(8,128)(2,1)}) %reduce-scatter.39.cloned.1.call-update) | async-done | bytes 110608 | tf_op jit(solution)/shard_map/reduce_scatter | solution.py:345
  984.3 39.2 %reduce-scatter.37.cloned.1.call-done = bf16[96,576]{1,0:T(8,128)(2,1)} async-done(((bf16[768,576]{1,0:T(8,128)(2,1)}), bf16[96,576]{1,0:T(8,128)(2,1)}) %reduce-scatter.37.cloned.1.call-update) | async-done | bytes 110608 | tf_op jit(solution)/shard_map/reduce_scatter | solution.py:345
  1025.2 35.8 %reduce-scatter.35.cloned.1.call-done = bf16[1,256,768]{2,1,0:T(8,128)(2,1)} async-done(((bf16[1,1024,768]{2,1,0:T(8,128)(2,1)}), bf16[1,256,768]{2,1,0:T(8,128)(2,1)}) %reduce-scatter.35.cloned.1.call-update) | async-done | bytes 393232 | tf_op jit(solution)/shard_map/reduce_scatter | solution.py:319
  1061.1 36.4 %reduce-scatter.33.cloned.1.call-done = bf16[1,256,768]{2,1,0:T(8,128)(2,1)} async-done(((bf16[1,1024,768]{2,1,0:T(8,128)(2,1)}), bf16[1,256,768]{2,1,0:T(8,128)(2,1)}) %reduce-scatter.33.cloned.1.call-update) | async-done | bytes 393232 | tf_op jit(solution)/shard_map/reduce_scatter | solution.py:316
  1099.3 39.9 %all-reduce.12 = (f32[768,2]{0,1:T(2,128)S(1)}, f32[768,2]{0,1:T(2,128)S(1)}, f32[768,4]{0,1:T(4,128)S(1)}, f32[768,4]{0,1:T(4,128)S(1)}) all-reduce(f32[768,2]{0,1:T(2,128)S(1)} %pad_maximum_fusion.8, f32[768,2]{0,1:T(2,128)S(1)} %pad_maximum_fusion.7, ...), channel_id=36, replica_groups=mesh['tensor'=4,'dp'=4,'ctx'=2] {'tensor','dp','ctx'}, use_global_device_ids=true, to_apply=%region_67.68.clone | all-reduce | flops 9216 | bytes 73728
  (477 shorter events, 339.5 us)
Async XLA Ops:
  7.2 69.3 %all-gather.34.cloned.1.call-start = ((), (), s32[]{:S(2)}) async-start(), calls=%async_computation.37 | async-start | bytes 1966080 | tf_op jit(solution)/shard_map/all_gather | solution.py:201
  7.9 75.7 %all-gather.36.cloned.1.call-start = ((), (), s32[]{:S(2)}) async-start(), calls=%async_computation.38 | async-start | bytes 1327104 | tf_op jit(solution)/shard_map/all_gather | solution.py:194
  9.7 93.4 %all-gather.38.cloned.1.call-start = ((), (), s32[]{:S(2)}) async-start(), calls=%async_computation.39 | async-start | bytes 1327104 | tf_op jit(solution)/shard_map/all_gather | solution.py:196
  11.5 120.9 %all-gather.24.cloned.1.call-start = ((), (), s32[]{:S(2)}) async-start(), calls=%async_computation.16 | async-start | bytes 2359296 | tf_op jit(solution)/shard_map/all_gather | solution.py:214
  34.3 170.4 %copy-start.41 = (f32[768]{0:T(1024)}, f32[768]{0:T(1024)S(1)}, u32[]{:S(2)}) copy-start(f32[768]{0:T(1024)S(1)} %get-tuple-element.510) | copy-start | bytes 9220
  34.3 170.4 %copy-start.43 = (f32[768]{0:T(1024)}, f32[768]{0:T(1024)S(1)}, u32[]{:S(2)}) copy-start(f32[768]{0:T(1024)S(1)} %get-tuple-element.511) | copy-start | bytes 9220
  34.3 212.4 %copy-start.74 = (f32[768]{0:T(1024)}, f32[768]{0:T(1024)S(1)}, u32[]{:S(2)}) copy-start(f32[768]{0:T(1024)S(1)} %get-tuple-element.509) | copy-start | bytes 9220
  35.7 211.0 %copy-start.49 = (f32[768]{0:T(1024)}, f32[768]{0:T(1024)S(1)}, u32[]{:S(2)}) copy-start(f32[768]{0:T(1024)S(1)} %get-tuple-element.514) | copy-start | bytes 9220
  83.4 121.3 %reduce-scatter.21.cloned.1.call-start = ((), (), s32[]{:S(2)}) async-start(), calls=%async_computation.17 | async-start | bytes 1966080 | tf_op jit(solution)/shard_map/reduce_scatter | solution.py:224
  153.1 89.8 %all-gather.26.cloned.1.call-start = ((), (), s32[]{:S(2)}) async-start(), calls=%async_computation.18 | async-start | bytes 1966080 | tf_op jit(solution)/shard_map/all_gather | solution.py:201
  206.6 74.3 %all-gather.30.cloned.1.call-start = ((), (), s32[]{:S(2)}) async-start(), calls=%async_computation.21 | async-start | bytes 1966080 | tf_op jit(solution)/shard_map/all_gather | solution.py:270
  208.1 101.1 %all-gather.28.cloned.1.call-start = ((), (), s32[]{:S(2)}) async-start(), calls=%async_computation.19 | async-start | bytes 2359296 | tf_op jit(solution)/shard_map/all_gather | solution.py:214
  250.2 114.5 %all-gather.40.cloned.1.call-start = ((), (), s32[]{:S(2)}) async-start(), calls=%async_computation.40 | async-start | bytes 1327104 | tf_op jit(solution)/shard_map/all_gather | solution.py:194
  250.9 125.8 %all-gather.42.cloned.1.call-start = ((), (), s32[]{:S(2)}) async-start(), calls=%async_computation.41 | async-start | bytes 1327104 | tf_op jit(solution)/shard_map/all_gather | solution.py:196
  251.5 192.2 %reduce-scatter.25.cloned.1.call-start = ((), (), s32[]{:S(2)}) async-start(), calls=%async_computation.22 | async-start | bytes 2359296 | tf_op jit(solution)/shard_map/reduce_scatter | solution.py:296
  364.7 116.7 %reduce-scatter.29.cloned.1.call-start = ((), (), s32[]{:S(2)}) async-start(), calls=%async_computation.24 | async-start | bytes 1966080 | tf_op jit(solution)/shard_map/reduce_scatter | solution.py:319
  386.6 131.5 %reduce-scatter.27.cloned.1.call-start = ((), (), s32[]{:S(2)}) async-start(), calls=%async_computation.23 | async-start | bytes 1966080 | tf_op jit(solution)/shard_map/reduce_scatter | solution.py:316
  449.9 110.9 %all-gather.32.cloned.1.call-start = ((), (), s32[]{:S(2)}) async-start(), calls=%async_computation.25 | async-start | bytes 1966080 | tf_op jit(solution)/shard_map/all_gather | solution.py:270
  524.6 150.8 %reduce-scatter.31.cloned.1.call-start = ((), (), s32[]{:S(2)}) async-start(), calls=%async_computation.26 | async-start | bytes 2359296 | tf_op jit(solution)/shard_map/reduce_scatter | solution.py:296
  607.8 105.1 %reduce-scatter.23.cloned.1.call-start = ((), (), s32[]{:S(2)}) async-start(), calls=%async_computation.20 | async-start | bytes 1966080 | tf_op jit(solution)/shard_map/reduce_scatter | solution.py:224
  619.2 129.1 %reduce-scatter.43.cloned.1.call-start = ((), (), s32[]{:S(2)}) async-start(), calls=%async_computation.32 | async-start | bytes 331776 | tf_op jit(solution)/shard_map/reduce_scatter | solution.py:351
  620.5 164.2 %reduce-scatter.41.cloned.1.call-start = ((), (), s32[]{:S(2)}) async-start(), calls=%async_computation.31 | async-start | bytes 331776 | tf_op jit(solution)/shard_map/reduce_scatter | solution.py:351
  623.2 201.5 %reduce-scatter.51.cloned.1.call-start = ((), (), s32[]{:S(2)}) async-start(), calls=%async_computation.36 | async-start | bytes 1327104 | tf_op jit(solution)/shard_map/reduce_scatter | solution.py:354
  627.2 237.7 %reduce-scatter.49.cloned.1.call-start = ((), (), s32[]{:S(2)}) async-start(), calls=%async_computation.35 | async-start | bytes 1327104 | tf_op jit(solution)/shard_map/reduce_scatter | solution.py:354
  631.7 273.2 %reduce-scatter.47.cloned.1.call-start = ((), (), s32[]{:S(2)}) async-start(), calls=%async_computation.34 | async-start | bytes 1327104 | tf_op jit(solution)/shard_map/reduce_scatter | solution.py:348
  636.1 309.2 %reduce-scatter.45.cloned.1.call-start = ((), (), s32[]{:S(2)}) async-start(), calls=%async_computation.33 | async-start | bytes 1327104 | tf_op jit(solution)/shard_map/reduce_scatter | solution.py:348
  647.0 337.3 %reduce-scatter.39.cloned.1.call-start = ((), (), s32[]{:S(2)}) async-start(), calls=%async_computation.30 | async-start | bytes 1105920 | tf_op jit(solution)/shard_map/reduce_scatter | solution.py:345
  651.6 371.8 %reduce-scatter.37.cloned.1.call-start = ((), (), s32[]{:S(2)}) async-start(), calls=%async_computation.29 | async-start | bytes 1105920 | tf_op jit(solution)/shard_map/reduce_scatter | solution.py:345
  680.9 380.1 %reduce-scatter.35.cloned.1.call-start = ((), (), s32[]{:S(2)}) async-start(), calls=%async_computation.28 | async-start | bytes 1966080 | tf_op jit(solution)/shard_map/reduce_scatter | solution.py:319
  685.4 412.1 %reduce-scatter.33.cloned.1.call-start = ((), (), s32[]{:S(2)}) async-start(), calls=%async_computation.27 | async-start | bytes 1966080 | tf_op jit(solution)/shard_map/reduce_scatter | solution.py:316
  694.0 403.5 %copy-start.12 = (f32[1,1024,768]{2,1,0:T(8,128)S(1)}, f32[1,1024,768]{2,1,0:T(8,128)}, u32[]{:S(2)}) copy-start(f32[1,1024,768]{2,1,0:T(8,128)} %fusion.114) | copy-start | bytes 9437188
  715.2 425.5 %copy-start.71 = (f32[256]{0:T(256)S(1)}, f32[256]{0:T(256)}, u32[]{:S(2)}) copy-start(f32[256]{0:T(256)} %dynamic_slice.78) | copy-start | bytes 3076
  (87 other events, 1612.2 us)
Sparse Core Ops, SparseCore 0:
  9.6 39.7 all-gather.33
  51.9 24.6 all-gather.35
  79.1 24.0 all-gather.37
  105.1 27.1 all-gather.23
  153.2 51.4 reduce-scatter.20
  206.7 36.0 all-gather.25
  245.0 35.9 all-gather.29
  283.1 26.0 all-gather.27
  311.1 24.0 all-gather.39
  336.9 24.0 all-gather.41
  364.8 78.9 reduce-scatter.24
  446.0 35.2 reduce-scatter.28
  483.7 34.2 reduce-scatter.26
  524.8 36.0 all-gather.31
  607.9 67.4 reduce-scatter.30
  677.6 35.2 reduce-scatter.22
  716.4 31.8 reduce-scatter.42
  751.8 32.8 reduce-scatter.40
  787.9 36.7 reduce-scatter.50
  828.1 36.7 reduce-scatter.48
  868.1 36.7 reduce-scatter.46
  908.5 36.7 reduce-scatter.44
  948.5 35.7 reduce-scatter.38
  987.7 35.7 reduce-scatter.36
  1025.7 35.2 reduce-scatter.34
  1063.2 34.2 reduce-scatter.32
where the time goes:
time: 1160 us; the launch traced here: 1150 us
  waiting for transfers between devices  689 us (59%)
  matrix products  200 us (17%)
  blocking collectives  145 us (12%)
  other arithmetic  66.4 us (6%)
  local copies, waits for them, and re-layouts  27.4 us (2%)
  between operations  18.5 us (2%)
    reduce_scatter x2, waiting for transfers between devices, shards(): lax.psum_scatter(grad_pairs.astype(jnp.bfloat16), 'ctx', scatter_dimensio...  80.8 us
    reduce_scatter x2, waiting for transfers between devices, shards(): lax.psum_scatter(grad_down_w.astype(jnp.bfloat16), ('dp', 'ctx'), scatter...  78.7 us
    reduce_scatter x2, waiting for transfers between devices, shards(): lax.psum_scatter(grad_up_w.astype(jnp.bfloat16), ('dp', 'ctx'), scatter_d...  78.6 us
    reduce_scatter x2, waiting for transfers between devices, shards(): lax.psum_scatter(grad_first.astype(jnp.bfloat16), 'tensor', scatter_dimen...  73.2 us
    unnamed x3, blocking collectives  70.4 us
    reduce_scatter x2, waiting for transfers between devices, shards(): lax.psum_scatter(branch.astype(jnp.bfloat16), 'tensor', scatter_dimension...  69.1 us
    reduce_scatter x2, waiting for transfers between devices, shards(): lax.psum_scatter(grad_dense_w.astype(jnp.bfloat16), ('dp', 'ctx'), scatte...  65.3 us
    reduce_scatter x2, waiting for transfers between devices, shards(): lax.psum_scatter(grad_second.astype(jnp.bfloat16), 'tensor', scatter_dime...  65 us
  transfers between devices with their start and end apart: 26, of which 22 were waited for; matrix products, arithmetic and copies ran while one was open for 18% of the time, Pallas kernels for 0%

commit v1 on v0

v1 whole, which is shorter than its diff:
```python
from functools import partial

import jax
import jax.numpy as jnp
from jax import lax
from jax.experimental import pallas as pl
from jax.experimental.pallas import tpu as pltpu
from jax.sharding import PartitionSpec as P

HEAD_DIM = 64
ROTARY = 16
LAYERS = 2
EPSILON = 1e-05
MASKED = -1e30
LANES = 128
SCALE = HEAD_DIM ** (-0.5)
FAR = 1 << 24
BF = jnp.bfloat16
F32 = jnp.float32
NT = (((1,), (1,)), ((), ()))


def dot(a, b):
    return jnp.dot(a, b, preferred_element_type=F32)


def dot_nt(a, b):
    return lax.dot_general(a, b, NT, preferred_element_type=F32)


def params(mib=56):
    return pltpu.CompilerParams(vmem_limit_bytes=mib << 20)


def z_gather(own):
    n = lax.axis_size("tensor")
    return [own] + [
        lax.ppermute(own, "tensor", [(s, (s - c) % n) for s in range(n)]) for c in range(1, n)
    ]


def z_scatter(parts):
    n = lax.axis_size("tensor")
    total = parts[0].astype(F32)
    for c in range(1, n):
        got = lax.ppermute(parts[c].astype(BF), "tensor", [(s, (s + c) % n) for s in range(n)])
        total = total + got.astype(F32)
    return total


def bits_of(axis):
    return lax.axis_size(axis).bit_length() - 1


def scatter_weights(value, first_y, wire=BF):
    nd, nc = lax.axis_size("dp"), lax.axis_size("ctx")
    kd, kc = bits_of("dp"), bits_of("ctx")
    if nd != 1 << kd or nc != 1 << kc:
        flat = value.astype(wire)
        return lax.psum_scatter(flat, ("dp", "ctx"), scatter_dimension=0, tiled=True)[0].astype(F32)
    labels = [("dp", b) for b in reversed(range(kd))] + [("ctx", b) for b in reversed(range(kc))]
    core = [("dp", 0)] if kd else []
    y_steps = [("dp", b) for b in range(1, kd)]
    x_steps = [("ctx", b) for b in range(kc)]
    order = core + (y_steps + x_steps if first_y else x_steps + y_steps)
    rest = value.shape[1:]
    value = value.reshape((2,) * (kd + kc) + rest)
    for axis, bit in order:
        dim = labels.index((axis, bit))
        mine = (lax.axis_index(axis) >> bit) & 1
        send = lax.dynamic_index_in_dim(value, 1 - mine, dim, keepdims=False).astype(wire)
        keep = lax.dynamic_index_in_dim(value, mine, dim, keepdims=False)
        size = lax.axis_size(axis)
        got = lax.ppermute(send, axis, [(s, s ^ (1 << bit)) for s in range(size)])
        value = keep + got.astype(F32)
        labels.pop(dim)
    return value


def rotated(tile, cosine, sine_a, sine_b):
    return tile * cosine + pltpu.roll(tile, LANES - 8, 1) * sine_a + pltpu.roll(tile, 8, 1) * sine_b


def unrotated(tile, cosine, sine_a, sine_b):
    return tile * cosine - pltpu.roll(tile, LANES - 8, 1) * sine_a - pltpu.roll(tile, 8, 1) * sine_b


def unit_of(x):
    values = x.astype(F32)
    centre = values - jnp.mean(values, axis=-1, keepdims=True)
    inverse = lax.rsqrt(jnp.mean(centre * centre, axis=-1, keepdims=True) + EPSILON)
    return centre * inverse


def entry_kernel(
    heads, x_ref, up_ref, mix_ref, bias_ref, vec_ref, cos_ref, sa_ref, sb_ref,
    first_ref, second_ref, q_ref, kv_ref, active_ref, slope_ref,
):
    width = x_ref.shape[-1]
    unit = unit_of(x_ref[0])
    first = (unit * vec_ref[0:1] + vec_ref[2:3]).astype(BF)
    second = (unit * vec_ref[1:2] + vec_ref[3:4]).astype(BF)
    first_ref[0] = first
    second_ref[0] = second
    mixw = mix_ref[...].reshape(width, -1)
    proj = dot(first, mixw) + bias_ref[1:2, : mixw.shape[1]]
    cosine, sine_a, sine_b = cos_ref[0], sa_ref[0], sb_ref[0]
    for h in range(heads):
        cols = slice(h * LANES, (h + 1) * LANES)
        kv_ref[0, :, cols] = rotated(proj[:, cols], cosine, sine_a, sine_b).astype(BF)
        qcols = slice((heads + h) * LANES, (heads + h + 1) * LANES)
        q_ref[0, :, cols] = (rotated(proj[:, qcols], cosine, sine_a, sine_b) * SCALE).astype(BF)
    upw = up_ref[...].reshape(width, -1)
    hidden = dot(second, upw) + bias_ref[0:1, : upw.shape[1]]
    half = 0.5 * (1.0 + lax.erf(hidden * (0.5**0.5)))
    active_ref[0] = (hidden * half).astype(BF)
    bell = jnp.exp(hidden * hidden * -0.5) * 0.3989422804014327
    slope_ref[0] = (half + hidden * bell).astype(BF)


def entry(xs, gathered, k, bias, vec, tables, heads):
    n, tokens, width = xs.shape
    shards = gathered.shape[0]
    ff = gathered.shape[2]
    wide = heads * LANES
    token = lambda w: pl.BlockSpec((1, tokens, w), lambda c: (c, 0, 0))
    whole = lambda a: pl.BlockSpec(a.shape, lambda c: (0,) * a.ndim)
    weight = lambda j: pl.BlockSpec((shards, k, ff), lambda c: (0, j, 0))
    out = lambda w: jax.ShapeDtypeStruct((n, tokens, w), BF)
    return pl.pallas_call(
        partial(entry_kernel, heads),
        grid=(n,),
        in_specs=[token(width), weight(0), weight(2), whole(bias), whole(vec)]
        + [token(LANES)] * 3,
        out_specs=[token(width), token(width), token(wide), token(wide), token(ff), token(ff)],
        out_shape=[out(width), out(width), out(wide), out(wide), out(ff), out(ff)],
        compiler_params=params(),
        name="entry",
    )(xs, gathered, gathered, bias, vec, *tables)


def load_pairs(kv_refs, kv_s):
    n = kv_refs[0].shape[0]
    for e, ref in enumerate(kv_refs):
        for c in range(n):
            kv_s[e * n + c] = ref[c, 0]


def allowed_pairs(base_ref, begin_ref, kb, c, n, blocks, shape):
    key_slot = base_ref[n + kb] + lax.broadcasted_iota(jnp.int32, shape, 0)
    query_slot = base_ref[c] + lax.broadcasted_iota(jnp.int32, shape, 1)
    return (key_slot >= begin_ref[0, c]) & (key_slot <= query_slot)


def attend_kernel(
    heads, extras, need_ref, base_ref, begin_ref, q_ref, *refs
):
    kv_refs = refs[: 1 + extras]
    mixed_ref, ot_ref, lse_ref, kv_s, vt_s, top_s, total_s, acc_s = refs[1 + extras :]
    n, _, count, _ = q_ref.shape
    blocks = n * (1 + extras)
    row = pl.program_id(0)
    load_pairs(kv_refs, kv_s)

    def turn(kb, _):
        for h in range(heads):
            tile = kv_s[kb, :, h * LANES : (h + 1) * LANES].astype(F32)
            vt_s[kb, h] = tile.T[HEAD_DIM:].astype(BF)
        return 0

    lax.fori_loop(0, blocks, turn, 0)

    def per_query(c, _):
        top_s[...] = jnp.full(top_s.shape, MASKED, F32)
        total_s[...] = jnp.zeros(total_s.shape, F32)
        acc_s[...] = jnp.zeros(acc_s.shape, F32)

        def per_key(kb, _):
            @pl.when(need_ref[row, c * blocks + kb] > 0)
            def _():
                allowed = allowed_pairs(
                    base_ref, begin_ref, kb, c, n, blocks, (count, count)
                )
                for h in range(heads):
                    cols = slice(h * LANES, (h + 1) * LANES)
                    scores = dot_nt(kv_s[kb, :, cols], q_ref[c, 0, :, cols])
                    scores = jnp.where(allowed, scores, MASKED)
                    old = top_s[h]
                    new = jnp.maximum(old, jnp.max(scores, axis=0, keepdims=True))
                    fade = jnp.exp(old - new)
                    weights = jnp.exp(scores - new)
                    top_s[h] = new
                    total_s[h] = total_s[h] * fade + jnp.sum(weights, axis=0, keepdims=True)
                    acc_s[h] = acc_s[h] * fade + dot(vt_s[kb, h], weights.astype(BF))

            return 0

        lax.fori_loop(0, blocks, per_key, 0)
        outs = []
        for h in range(heads):
            total = total_s[h]
            outs.append(acc_s[h] / total)
            lse_ref[0, c, h : h + 1] = top_s[h] + jnp.log(total)
        whole = jnp.concatenate(outs, axis=0)
        ot_ref[0, c] = whole
        mixed_ref[c, 0] = whole.T.astype(BF)
        return 0

    lax.fori_loop(0, n, per_query, 0)


def attention_specs(q, extras):
    n, rows, count, wide = q.shape
    smem = pl.BlockSpec(memory_space=pltpu.SMEM)
    begin = pl.BlockSpec((1, n, 1, count), lambda r: (r, 0, 0, 0))
    tokens = pl.BlockSpec((n, 1, count, wide), lambda r: (0, r, 0, 0))
    return n, rows, count, wide, smem, begin, tokens


def attend(need, base, begin, q, kvs, heads):
    extras = len(kvs) - 1
    n, rows, count, wide, smem, begin_spec, tokens = attention_specs(q, extras)
    blocks = n * (1 + extras)
    narrow = heads * HEAD_DIM
    return pl.pallas_call(
        partial(attend_kernel, heads, extras),
        grid=(rows,),
        in_specs=[smem, smem, begin_spec, tokens] + [tokens] * (1 + extras),
        out_specs=[
            pl.BlockSpec((n, 1, count, narrow), lambda r: (0, r, 0, 0)),
            pl.BlockSpec((1, n, narrow, count), lambda r: (r, 0, 0, 0)),
            pl.BlockSpec((1, n, heads, count), lambda r: (r, 0, 0, 0)),
        ],
        out_shape=[
            jax.ShapeDtypeStruct((n, rows, count, narrow), BF),
            jax.ShapeDtypeStruct((rows, n, narrow, count), F32),
            jax.ShapeDtypeStruct((rows, n, heads, count), F32),
        ],
        scratch_shapes=[
            pltpu.VMEM((blocks, count, wide), BF),
            pltpu.VMEM((blocks, heads, HEAD_DIM, count), BF),
            pltpu.VMEM((heads, 1, count), F32),
            pltpu.VMEM((heads, 1, count), F32),
            pltpu.VMEM((heads, HEAD_DIM, count), F32),
        ],
        compiler_params=params(),
        name="attend",
    )(need, base, begin, q, *kvs)


def attend_back_kernel(
    heads, extras, need_ref, base_ref, begin_ref, q_ref, do_ref, lse_ref, ot_ref, *refs
):
    kv_refs = refs[: 1 + extras]
    dq_ref = refs[1 + extras]
    dkv_refs = refs[2 + extras : 3 + 2 * extras]
    kv_s, kt_s, dkv_s, dqt_s, delta_s = refs[3 + 2 * extras :]
    n, _, count, _ = q_ref.shape
    blocks = n * (1 + extras)
    row = pl.program_id(0)
    load_pairs(kv_refs, kv_s)

    def turn(kb, _):
        for h in range(heads):
            tile = kv_s[kb, :, h * LANES : (h + 1) * LANES].astype(F32)
            kt_s[kb, h] = tile.T[:HEAD_DIM].astype(BF)
        dkv_s[kb] = jnp.zeros(dkv_s.shape[1:], F32)
        return 0

    lax.fori_loop(0, blocks, turn, 0)

    def per_query(c, _):
        dqt_s[...] = jnp.zeros(dqt_s.shape, F32)
        for h in range(heads):
            cols = slice(h * LANES, (h + 1) * LANES)
            dot_t = do_ref[c, 0, :, cols].astype(F32).T[HEAD_DIM:]
            out_t = ot_ref[0, c, h * HEAD_DIM : (h + 1) * HEAD_DIM]
            delta_s[h] = jnp.sum(dot_t * out_t, axis=0, keepdims=True)

        def per_key(kb, _):
            @pl.when(need_ref[row, c * blocks + kb] > 0)
            def _():
                allowed = allowed_pairs(
                    base_ref, begin_ref, kb, c, n, blocks, (count, count)
                )
                for h in range(heads):
                    cols = slice(h * LANES, (h + 1) * LANES)
                    pair = kv_s[kb, :, cols]
                    query = q_ref[c, 0, :, cols]
                    grad = do_ref[c, 0, :, cols]
                    scores = jnp.where(allowed, dot_nt(pair, query), MASKED)
                    probs = jnp.exp(scores - lse_ref[0, c, h : h + 1])
                    steps = probs * (dot_nt(pair, grad) - delta_s[h])
                    steps = steps.astype(BF)
                    dqt_s[h] += dot(kt_s[kb, h], steps)
                    dkv_s[kb, :, cols] += dot(steps, query) + dot(probs.astype(BF), grad)

            return 0

        lax.fori_loop(0, blocks, per_key, 0)
        for h in range(heads):
            tile = jnp.concatenate([dqt_s[h], jnp.zeros((HEAD_DIM, count), F32)], axis=0)
            dq_ref[c, 0, :, h * LANES : (h + 1) * LANES] = tile.T * SCALE
        return 0

    lax.fori_loop(0, n, per_query, 0)
    for e, ref in enumerate(dkv_refs):
        for c in range(n):
            ref[c, 0] = dkv_s[e * n + c].astype(ref.dtype)


def attend_back(need, base, begin, q, do, lse, ot, kvs, heads):
    extras = len(kvs) - 1
    n, rows, count, wide, smem, begin_spec, tokens = attention_specs(q, extras)
    blocks = n * (1 + extras)
    narrow = heads * HEAD_DIM
    return pl.pallas_call(
        partial(attend_back_kernel, heads, extras),
        grid=(rows,),
        in_specs=[smem, smem, begin_spec, tokens, tokens]
        + [
            pl.BlockSpec((1, n, heads, count), lambda r: (r, 0, 0, 0)),
            pl.BlockSpec((1, n, narrow, count), lambda r: (r, 0, 0, 0)),
        ]
        + [tokens] * (1 + extras),
        out_specs=[tokens] * (2 + extras),
        out_shape=[jax.ShapeDtypeStruct(q.shape, F32)] * 2
        + [jax.ShapeDtypeStruct(q.shape, BF)] * extras,
        scratch_shapes=[
            pltpu.VMEM((blocks, count, wide), BF),
            pltpu.VMEM((blocks, heads, HEAD_DIM, count), BF),
            pltpu.VMEM((blocks, count, wide), F32),
            pltpu.VMEM((heads, HEAD_DIM, count), F32),
            pltpu.VMEM((heads, 1, count), F32),
        ],
        compiler_params=params(),
        name="attend_back",
    )(need, base, begin, q, do, lse, ot, *kvs)


def feed_back_kernel(
    g_ref, x_ref, slope_ref, up_ref, down_ref, vec_ref, gh_ref, scaled_ref, sums_ref
):
    width = g_ref.shape[-1]

    @pl.when(pl.program_id(0) == 0)
    def _():
        sums_ref[...] = jnp.zeros(sums_ref.shape, F32)

    down = down_ref[...].reshape(-1, width)
    grad_hidden = (dot_nt(g_ref[0], down) * slope_ref[0].astype(F32)).astype(BF)
    gh_ref[0] = grad_hidden
    grad_second = dot_nt(grad_hidden, up_ref[...].reshape(width, -1))
    unit = unit_of(x_ref[0])
    sums_ref[0:1] += jnp.sum(grad_second * unit, axis=0, keepdims=True)
    sums_ref[1:2] += jnp.sum(grad_second, axis=0, keepdims=True)
    sums_ref[2:3] += jnp.sum(grad_hidden.astype(F32), axis=0, keepdims=True)
    scaled_ref[0] = grad_second * vec_ref[1:2]


def feed_back(g, xs, slope, gathered, k, vec):
    n, tokens, width = g.shape
    shards, _, ff = gathered.shape
    token = lambda w: pl.BlockSpec((1, tokens, w), lambda c: (c, 0, 0))
    weight = lambda j: pl.BlockSpec((shards, k, ff), lambda c: (0, j, 0))
    fixed = pl.BlockSpec((8, width), lambda c: (0, 0))
    return pl.pallas_call(
        feed_back_kernel,
        grid=(n,),
        in_specs=[token(width), token(width), token(ff), weight(0), weight(1), fixed],
        out_specs=[token(ff), token(width), fixed],
        out_shape=[
            jax.ShapeDtypeStruct((n, tokens, ff), BF),
            jax.ShapeDtypeStruct((n, tokens, width), F32),
            jax.ShapeDtypeStruct((8, width), F32),
        ],
        compiler_params=params(),
        name="feed_back",
    )(g, xs, slope, gathered, gathered, vec)


def exit_kernel(
    heads, extras, dq_ref, dkv_ref, *refs
):
    got_refs = refs[:extras]
    cos_ref, sa_ref, sb_ref, x_ref, mix_ref, vec_ref, scaled_ref, gp_ref, part_ref, sums_ref = refs[
        extras:
    ]
    width = x_ref.shape[-1]

    @pl.when(pl.program_id(0) == 0)
    def _():
        sums_ref[...] = jnp.zeros(sums_ref.shape, F32)

    cosine, sine_a, sine_b = cos_ref[0], sa_ref[0], sb_ref[0]
    for h in range(heads):
        cols = slice(h * LANES, (h + 1) * LANES)
        pair = dkv_ref[0, :, cols]
        for ref in got_refs:
            pair = pair + ref[0, :, cols].astype(F32)
        gp_ref[0, :, cols] = unrotated(pair, cosine, sine_a, sine_b).astype(BF)
        qcols = slice((heads + h) * LANES, (heads + h + 1) * LANES)
        gp_ref[0, :, qcols] = unrotated(dq_ref[0, :, cols], cosine, sine_a, sine_b).astype(BF)
    gp = gp_ref[0]
    grad_first = dot_nt(gp, mix_ref[...].reshape(width, -1))
    unit = unit_of(x_ref[0])
    sums_ref[0:1] += jnp.sum(grad_first * unit, axis=0, keepdims=True)
    sums_ref[1:2] += jnp.sum(grad_first, axis=0, keepdims=True)
    sums_ref[2:3] += jnp.sum(gp.astype(F32), axis=0, keepdims=True)
    part_ref[0] = (grad_first * vec_ref[0:1] + scaled_ref[0]).astype(BF)


def exit_pass(dq, dkv, got, tables, xs, gathered, k, vec, scaled, heads):
    n, tokens, width = xs.shape
    shards, _, ff = gathered.shape
    wide = heads * LANES
    token = lambda w: pl.BlockSpec((1, tokens, w), lambda c: (c, 0, 0))
    weight = lambda j: pl.BlockSpec((shards, k, ff), lambda c: (0, j, 0))
    fixed = pl.BlockSpec((8, width), lambda c: (0, 0))
    flat = lambda a: a.reshape(n, tokens, wide)
    return pl.pallas_call(
        partial(exit_kernel, heads, len(got)),
        grid=(n,),
        in_specs=[token(wide)] * (2 + len(got))
        + [token(LANES)] * 3
        + [token(width), weight(2), fixed, token(width)],
        out_specs=[token(2 * wide), token(width), fixed],
        out_shape=[
            jax.ShapeDtypeStruct((n, tokens, 2 * wide), BF),
            jax.ShapeDtypeStruct((n, tokens, width), BF),
            jax.ShapeDtypeStruct((8, width), F32),
        ],
        compiler_params=params(),
        name="exit_pass",
    )(flat(dq), flat(dkv), *[flat(a) for a in got], *tables, xs, gathered, vec, scaled)


def mix_columns(weight, heads):
    lead = weight.shape[:-1]
    split = weight.reshape(lead + (heads, 3, HEAD_DIM))
    pairs = split[..., 1:, :].reshape(lead + (heads * LANES,))
    query = jnp.concatenate([split[..., 0, :], jnp.zeros_like(split[..., 0, :])], axis=-1)
    return jnp.concatenate([pairs, query.reshape(lead + (heads * LANES,))], axis=-1)


def unmix_columns(grad, heads):
    lead = grad.shape[:-1]
    split = grad.reshape(lead + (2, heads, 2, HEAD_DIM))
    order = [split[..., 1, :, 0, :], split[..., 0, :, 0, :], split[..., 0, :, 1, :]]
    return jnp.stack(order, axis=-2).reshape(lead + (heads * 3 * HEAD_DIM,))


def pack_layer(mix_w, mix_b, dense_w, up_w, up_b, down_w, heads):
    width = up_w.shape[1]
    mix = mix_columns(mix_w, heads)
    wide = lambda v: jnp.pad(v, (0, width - v.shape[0]))[None]
    rows = [up_w, down_w, jnp.pad(mix, ((0, 0), (0, width - mix.shape[1]))), dense_w]
    rows += [wide(up_b), wide(mix_b)]
    total = sum(r.shape[0] for r in rows)
    rows.append(jnp.zeros((-total % 8, width), up_w.dtype))
    return jnp.concatenate(rows, axis=0)


def shards(
    block_input, seq_lengths, project_weight, project_bias, dense_weight, up_weight, up_bias,
    down_weight, norm_gains, shift_vectors, cotangent,
):
    rows, _, own_count, width = block_input.shape
    n = lax.axis_size("tensor")
    places = lax.axis_size("ctx")
    extras = places - 1
    place = lax.axis_index("ctx")
    me = lax.axis_index("tensor")
    block_len = own_count * n
    tokens = rows * own_count
    heads = project_weight.shape[2] // (3 * HEAD_DIM)
    wide = heads * LANES
    k_rows = up_weight.shape[1]
    d_rows = dense_weight.shape[1]
    f_own = up_bias.shape[1]
    m_own = project_bias.shape[1]
    shard_count = lax.axis_size("dp") * places

    ends = jnp.cumsum(seq_lengths, axis=1)
    order = (me + jnp.arange(n, dtype=jnp.int32)) % n
    query_base = place * block_len + order * own_count
    slots = query_base[:, None] + jnp.arange(own_count, dtype=jnp.int32)[None]
    passed = (ends[:, None, None, :] <= slots[None, :, :, None]).astype(jnp.int32)
    begin = jnp.sum(passed * seq_lengths[:, None, None, :], axis=3)
    position = (slots[None] - begin).transpose(1, 0, 2).reshape(-1)
    frequency = 1.0 / 10000.0 ** (jnp.arange(0, ROTARY, 2, dtype=F32) / ROTARY)
    angle = frequency[:, None] * position.astype(F32)[None, :]
    cosine, sine = lax.optimization_barrier((jnp.cos(angle), jnp.sin(angle)))
    cosine, sine = cosine.T, sine.T
    ones = jnp.ones((cosine.shape[0], LANES - ROTARY), F32)
    zero8 = jnp.zeros_like(sine)
    tables = (
        jnp.concatenate([cosine, cosine, ones], axis=1).reshape(n, tokens, LANES),
        jnp.concatenate([-sine, zero8, ones * 0.0], axis=1).reshape(n, tokens, LANES),
        jnp.concatenate([zero8, sine, ones * 0.0], axis=1).reshape(n, tokens, LANES),
    )
    key_base = jnp.concatenate(
        [
            jnp.where(place >= e, (place - e) * block_len + order * own_count, FAR)
            for e in range(places)
        ]
    )
    base = jnp.concatenate([query_base, key_base])
    need = (key_base[None, None, :] <= query_base[None, :, None] + own_count - 1) & (
        key_base[None, None, :] + own_count - 1 >= begin[:, :, :1]
    )
    need = need.astype(jnp.int32).reshape(rows, -1)
    begin = begin.reshape(rows, n, 1, own_count)

    gains = norm_gains.astype(F32)
    shifts = shift_vectors.astype(F32)
    packed = [
        pack_layer(
            project_weight[l], project_bias[l], dense_weight[l], up_weight[l], up_bias[l],
            down_weight[l], heads,
        )
        for l in range(LAYERS)
    ]
    gathered = [
        lax.all_gather(packed[l], ("dp", "ctx"), axis=0, tiled=False) for l in range(LAYERS)
    ]
    vecs, biases, dense_ws, down_ws = [], [], [], []
    for l in range(LAYERS):
        full = gathered[l]
        vec = jnp.concatenate([gains[l].T, shifts[l].T, jnp.zeros((2, width), F32)], axis=0)
        vecs.append(vec)
        b_row = 3 * k_rows + d_rows
        up_b = full[:, b_row, :f_own].reshape(-1).astype(F32)
        mix_b = mix_columns(full[:, b_row + 1, :m_own].reshape(-1).astype(F32), heads)
        size = max(up_b.shape[0], mix_b.shape[0])
        biases.append(
            jnp.stack([jnp.pad(up_b, (0, size - up_b.shape[0])), jnp.pad(mix_b, (0, size - mix_b.shape[0]))])
        )
        dense_ws.append(full[:, 3 * k_rows : 3 * k_rows + d_rows].reshape(-1, width))
        down_ws.append(full[:, k_rows : 2 * k_rows].reshape(-1, width))

    flat = lambda a: a.reshape(n * tokens, -1)
    by_row = lambda a: a.reshape(n, rows, own_count, -1)
    stack = lambda chunks: jnp.stack(chunks)
    residual = block_input[:, 0].reshape(tokens, width).astype(F32)
    sent = block_input[:, 0].reshape(tokens, width)
    cot = cotangent[:, 0].reshape(tokens, width)
    stored = []
    for l in range(LAYERS):
        xs = stack(z_gather(sent))
        first, second, q, kv, active, slope = entry(
            xs, gathered[l], k_rows, biases[l], vecs[l], tables, heads
        )
        q, kv = by_row(q), by_row(kv)
        kvs = [kv] + [
            lax.ppermute(kv, "ctx", [(s, s + e) for s in range(places - e)])
            for e in range(1, places)
        ]
        mixed, ot, lse = attend(need, base, begin, q, kvs, heads)
        mixed = flat(mixed)
        branch = (dot(mixed, dense_ws[l]) + dot(flat(active), down_ws[l])).astype(BF)
        branch = branch.reshape(n, tokens, width)
        share = z_scatter([branch[c] for c in range(n)])
        residual = residual + share + shifts[l, :, 2] + shifts[l, :, 3]
        sent = residual.astype(BF)
        stored.append((xs, first, second, q, kvs, active, slope, mixed, ot, lse))

    grad = cot
    weight_out, small = [None] * LAYERS, [None] * LAYERS
    for l in reversed(range(LAYERS)):
        xs, first, second, q, kvs, active, slope, mixed, ot, lse = stored[l]
        gs = stack(z_gather(grad.astype(BF)))
        gf = flat(gs)
        token_sum = jnp.sum(grad, axis=0)
        gh, scaled, sums_b = feed_back(gs, xs, slope, gathered[l], k_rows, vecs[l])
        dense_pad = jnp.pad(
            dense_ws[l].reshape(heads, HEAD_DIM, width), ((0, 0), (HEAD_DIM, 0), (0, 0))
        ).reshape(wide, width)
        do = dot_nt(gf, dense_pad).astype(BF)
        dq, dkv, *send_back = attend_back(
            need, base, begin, q, by_row(do), lse, ot, kvs, heads
        )
        got = [
            lax.ppermute(send_back[e - 1], "ctx", [(s, s - e) for s in range(e, places)])
            for e in range(1, places)
        ]
        gp, part, sums_a = exit_pass(
            dq, dkv, got, tables, xs, gathered[l], k_rows, vecs[l], scaled, heads
        )
        summed = z_scatter([part[c] for c in range(n)])
        tn = lambda a, b: lax.dot_general(
            flat(a), flat(b), (((0,), (0,)), ((), ())), preferred_element_type=F32
        )
        down_g = tn(active, gs).reshape(shard_count, -1, width)
        up_g = tn(second, gh).reshape(shard_count, k_rows, -1)
        up_bg = jnp.pad(
            sums_b[2].reshape(shard_count, 1, -1), ((0, 0), (0, 7), (0, up_g.shape[2] - f_own))
        )
        dense_g = tn(mixed, gs).reshape(shard_count, d_rows, width)
        mix_g = tn(first, gp).reshape(shard_count, k_rows, -1)
        mix_bg = unmix_columns(sums_a[2, : 2 * wide], heads)
        mix_bg = jnp.pad(
            mix_bg.reshape(shard_count, 1, -1), ((0, 0), (0, 7), (0, width - m_own))
        )
        up_all = scatter_weights(jnp.concatenate([up_g, up_bg], axis=1), False)
        down_s = scatter_weights(down_g, True)
        mix_s = scatter_weights(mix_g, True)
        dense_all = scatter_weights(jnp.concatenate([dense_g, mix_bg], axis=1), False)
        weight_out[l] = (
            unmix_columns(mix_s, heads),
            dense_all[d_rows, :m_own],
            dense_all[:d_rows],
            up_all[:k_rows],
            up_all[k_rows, :f_own],
            down_s,
        )
        small[l] = jnp.stack([sums_a[0], sums_b[0], sums_a[1], sums_b[1], token_sum])
        unit_own = unit_of(xs[0])
        inverse = lax.rsqrt(jnp.var(xs[0].astype(F32), axis=-1, keepdims=True) + EPSILON)
        mean_s = jnp.mean(summed, axis=-1, keepdims=True)
        mean_su = jnp.mean(summed * unit_own, axis=-1, keepdims=True)
        grad = grad + inverse * (summed - mean_s - unit_own * mean_su)

    sums = jnp.stack(small)
    own_cols = width // (n * shard_count)
    sums = sums.reshape(LAYERS * 5, n, shard_count, own_cols).transpose(1, 2, 0, 3)
    pieces = [lax.dynamic_index_in_dim(sums, (me + c) % n, 0, keepdims=False) for c in range(n)]
    total = pieces[0]
    for c in range(1, n):
        total = total + lax.ppermute(pieces[c], "tensor", [(s, (s + c) % n) for s in range(n)])
    total = scatter_weights(total, False, F32).reshape(LAYERS, 5, own_cols)
    gains_out = total[:, :2].transpose(0, 2, 1)
    shifts_out = jnp.stack([total[:, 2], total[:, 3], total[:, 4], total[:, 4]], axis=-1)
    outs = [jnp.stack([weight_out[l][j] for l in range(LAYERS)]) for j in range(6)]
    shape = (rows, 1, own_count, width)
    return (residual.reshape(shape), grad.reshape(shape), *outs, gains_out, shifts_out)


def solution(mesh):
    in_specs = (
        P("dp", "ctx", "tensor", None),
        P("dp", None),
        P(None, ("dp", "ctx"), "tensor"),
        P(None, ("tensor", "dp", "ctx")),
        P(None, ("tensor", "dp", "ctx"), None),
        P(None, ("dp", "ctx"), "tensor"),
        P(None, ("tensor", "dp", "ctx")),
        P(None, ("tensor", "dp", "ctx"), None),
        P(),
        P(),
        P("dp", "ctx", "tensor", None),
    )
    out_specs = (
        P("dp", "ctx", "tensor", None),
        P("dp", "ctx", "tensor", None),
        P(None, ("dp", "ctx"), "tensor"),
        P(None, ("tensor", "dp", "ctx")),
        P(None, ("tensor", "dp", "ctx"), None),
        P(None, ("dp", "ctx"), "tensor"),
        P(None, ("tensor", "dp", "ctx")),
        P(None, ("tensor", "dp", "ctx"), None),
        P(None, ("tensor", "dp", "ctx"), None),
        P(None, ("tensor", "dp", "ctx"), None),
    )
    return jax.shard_map(shards, mesh=mesh, in_specs=in_specs, out_specs=out_specs, check_vma=False)
```

time: 1160 us -> 640 us (0.55)
  waiting for transfers between devices: 689 us -> 203 us
  matrix products: 200 us -> 30 us
  blocking collectives: 145 us -> 0 us
  starting transfers between devices: 1.86 us -> 145 us
  Pallas kernels: 0 us -> 110 us
  local copies, waits for them, and re-layouts: 27.4 us -> 78.1 us
  other arithmetic: 66.4 us -> 49.7 us
    reduce_scatter x16 -> x0, waiting for transfers between devices: 571 us -> none  [the longest x2 80.8 us: shards(): lax.psum_scatter(grad_pairs.astype(jnp.bfloat16), 'ctx', scatter_dimensio...]
    dot_general x42 -> x14, matrix products: 200 us -> 30 us  [the longest x8 16.8 us: shards(): lax.dot_general(flat(a), flat(b), (((0,), (0,)), ((), ())), preferred_ele...]
    ppermute x0 -> x58, waiting for transfers between devices: none -> 164 us  [the longest x12 56.4 us: z_gather(): lax.ppermute(own, 'tensor', [(s, (s - c) % n) for s in range(n)])]
    ppermute x0 -> x58, starting transfers between devices: none -> 145 us  [the longest x27 66.3 us: scatter_weights(): got = lax.ppermute(send, axis, [(s, s ^ 1 << bit) for s in range(size)])]
    pallas_call x0 -> x10, Pallas kernels: none -> 110 us  [the longest x2 34.4 us: attend_back(): pl.pallas_call(partial(attend_back_kernel, heads, extras), grid=(rows,),...]
    all_gather x10 -> x2, waiting for transfers between devices: 116 us -> 39 us  [shards(): lax.all_gather(packed[l], ('dp', 'ctx'), axis=0, tiled=False)]
    all_gather x4 -> x0, blocking collectives: 74.6 us -> none  [the longest x2 38.6 us: shards(): lax.all_gather(project_weight[layer], ('dp', 'ctx'), axis=0, tiled=True)]
    unnamed x3 -> x0, blocking collectives: 70.4 us -> none
  transfers between devices with their start and end apart: 26 -> 60, of which waited for: 22 -> 23; matrix products, arithmetic and copies ran while one was open for 18% -> 21% of each run, Pallas kernels for 0% -> 13%
where the time goes in v1:
time: 640 us; the launch traced here: 632 us
  waiting for transfers between devices  203 us (32%)
  starting transfers between devices  145 us (23%)
  Pallas kernels  110 us (17%)
  local copies, waits for them, and re-layouts  78.1 us (12%)
  other arithmetic  49.7 us (8%)
  matrix products  30 us (5%)
  between operations  16.2 us (3%)
    ppermute x27, starting transfers between devices, scatter_weights(): got = lax.ppermute(send, axis, [(s, s ^ 1 << bit) for s in range(size)])  66.3 us
    ppermute x12, waiting for transfers between devices, z_gather(): lax.ppermute(own, 'tensor', [(s, (s - c) % n) for s in range(n)])  56.4 us
    ppermute x27, waiting for transfers between devices, scatter_weights(): got = lax.ppermute(send, axis, [(s, s ^ 1 << bit) for s in range(size)])  53.9 us
    ppermute x12, waiting for transfers between devices, z_scatter(): lax.ppermute(parts[c].astype(BF), 'tensor', [(s, (s + c) % n) for s in ra...  53.1 us
    all_gather x2, waiting for transfers between devices, shards(): lax.all_gather(packed[l], ('dp', 'ctx'), axis=0, tiled=False)  39 us
    pallas_call x2, Pallas kernels, attend_back(): pl.pallas_call(partial(attend_back_kernel, heads, extras), grid=(rows,),...  34.4 us
    pallas_call x2, Pallas kernels, attend(): pl.pallas_call(partial(attend_kernel, heads, extras), grid=(rows,), in_sp...  27.9 us
    ppermute x12, starting transfers between devices, z_scatter(): lax.ppermute(parts[c].astype(BF), 'tensor', [(s, (s + c) % n) for s in ra...  24 us
  transfers between devices with their start and end apart: 60, of which 23 were waited for; matrix products, arithmetic and copies ran while one was open for 21% of the time, Pallas kernels for 13%

profile of v1, /device:TPU:0, one launch (start us, length us, event | category | flops | bytes accessed | tf_op | source)
XLA Modules:
  0.0 632.0 jit_solution(4077594426727335102)
XLA Ops:
  35.3 12.3 %collective-permute-done.1 = bf16[256,768]{1,0:T(8,128)(2,1)S(1)} collective-permute-done((bf16[256,768]{1,0:T(8,128)(2,1)S(1)}, bf16[256,768]{1,0:T(8,128)(2,1)S(1)}, u32[]{:S(2)}, u32[]{:S(2)}) %collective-permute-start.1) | collective-permute-done | bytes 393248 | tf_op jit(solution)/shard_map/ppermute | solution.py:38
  50.9 38.1 %all-gather.7.cloned.1.call-done = bf16[2560,768]{1,0:T(8,128)(2,1)} async-done(((bf16[320,768]{1,0:T(8,128)(2,1)}), bf16[2560,768]{1,0:T(8,128)(2,1)}) %all-gather.7.cloned.1.call-update) | async-done | bytes 3932176 | tf_op jit(solution)/shard_map/all_gather | solution.py:525
  92.6 8.5 %entry.2 = (bf16[4,256,768]{2,1,0:T(8,128)(2,1)}, bf16[4,256,768]{2,1,0:T(8,128)(2,1)}, bf16[4,256,384]{2,1,0:T(8,128)(2,1)}, bf16[4,256,384]{2,1,0:T(8,128)(2,1...) custom-call(bf16[4,256,768]{2,1,0:T(8,128)(2,1)} %pad_maximum_fusion.x_ref.refs_4_, ...), custom_call_target="tpu_custom_call" | custom-call | tf_op jit(solution)/shard_map/entry/pallas_call | solution.py:130
  101.1 3.6 collective-permute-start.3
  129.9 14.0 %attend.2 = (bf16[4,1,256,192]{3,2,1,0:T(8,128)(2,1)}, f32[1,4,192,256]{3,2,1,0:T(8,128)}, f32[1,4,3,256]{3,2,1,0:T(4,128)}) custom-call(s32[1,32]{1,0:T(1,128)} %and_convert_fusion.need_ref, s32[12]{0:T(128)} %pad_add_fusion.1.base_ref, s32[1,4,1,256]{3,2,1,0:T(1,128)} %reshape.577.begin_ref, bf16[4,1,256,384]{3,2,1,0:T(8,128)(2,1)} %bitcast.508, ...), custom_call_target="tpu_custom_call" | custom-call | tf_op jit(solution)/shard_map/attend/pallas_call | solution.py:225
  146.6 3.4 collective-permute-start.6
  155.5 4.3 collective-permute-done.6
  159.8 24.3 %collective-permute-done.5 = bf16[256,768]{1,0:T(8,128)(2,1)} collective-permute-done((bf16[256,768]{1,0:T(8,128)(2,1)}, bf16[256,768]{1,0:T(8,128)(2,1)}, u32[]{:S(2)}, u32[]{:S(2)}) %collective-permute-start.5) | collective-permute-done | bytes 393248 | tf_op jit(solution)/shard_map/ppermute | solution.py:46
  193.0 6.9 %collective-permute-done.9 = bf16[256,768]{1,0:T(8,128)(2,1)S(1)} collective-permute-done((bf16[256,768]{1,0:T(8,128)(2,1)S(1)}, bf16[256,768]{1,0:T(8,128)(2,1)S(1)}, u32[]{:S(2)}, u32[]{:S(2)}) %collective-permute-start.9) | collective-permute-done | bytes 393248 | tf_op jit(solution)/shard_map/ppermute | solution.py:38
  199.9 15.0 %collective-permute-done.8 = bf16[256,768]{1,0:T(8,128)(2,1)S(1)} collective-permute-done((bf16[256,768]{1,0:T(8,128)(2,1)S(1)}, bf16[256,768]{1,0:T(8,128)(2,1)S(1)}, u32[]{:S(2)}, u32[]{:S(2)}) %collective-permute-start.8) | collective-permute-done | bytes 393248 | tf_op jit(solution)/shard_map/ppermute | solution.py:38
  216.3 8.4 %entry.3 = (bf16[4,256,768]{2,1,0:T(8,128)(2,1)}, bf16[4,256,768]{2,1,0:T(8,128)(2,1)}, bf16[4,256,384]{2,1,0:T(8,128)(2,1)}, bf16[4,256,384]{2,1,0:T(8,128)(2,1...) custom-call(bf16[4,256,768]{2,1,0:T(8,128)(2,1)} %pad_maximum_fusion.1.x_ref.refs_4_, ...), custom_call_target="tpu_custom_call" | custom-call | tf_op jit(solution)/shard_map/entry/pallas_call | solution.py:130
  224.7 17.6 %collective-permute-start.10 = (bf16[4,1,256,384]{3,2,1,0:T(8,128)(2,1)}, bf16[4,1,256,384]{3,2,1,0:T(8,128)(2,1)S(1)}, u32[]{:S(2)}, u32[]{:S(2)}) collective-permute-start(bf16[4,1,256,384]{3,2,1,0:T(8,128)(2,1)} %bitcast.515), channel_id=1, source_target_pairs={{0,1},{2,3},{4,5},{6,7},{8,9},{10,11},{12,13},{14,15},{16,17},{18,... | collective-permute-start | bytes 2359304 | tf_op jit(solution)/shard_map/ppermute | solution.py:556
  242.3 7.6 %feed_back.2 = (bf16[4,256,768]{2,1,0:T(8,128)(2,1)}, f32[4,256,768]{2,1,0:T(8,128)}, f32[8,768]{1,0:T(8,128)}) custom-call(bf16[4,256,768]{2,1,0:T(8,128)(2,1)} %copy-done, bf16[4,256,768]{2,1,0:T(8,128)(2,1)} %pad_maximum_fusion.1.x_ref.refs_4_, bf16[4,256,768]{2,1,0:T(8,128)(2,1)} %get-tuple-element.64.slope_ref, bf16[8,320,768]{2,1,0:T(8,128)(2,1)} %bitcast.477, ...), custom_call_target="tpu_custom_call" | custom-call | tf_op jit(solution)/shard_map/feed_back/pallas_call | solution.py:367
  277.0 14.0 %attend.3 = (bf16[4,1,256,192]{3,2,1,0:T(8,128)(2,1)}, f32[1,4,192,256]{3,2,1,0:T(8,128)}, f32[1,4,3,256]{3,2,1,0:T(4,128)}) custom-call(s32[1,32]{1,0:T(1,128)} %and_convert_fusion.need_ref, s32[12]{0:T(128)} %pad_add_fusion.1.base_ref, s32[1,4,1,256]{3,2,1,0:T(1,128)} %reshape.577.begin_ref, bf16[4,1,256,384]{3,2,1,0:T(8,128)(2,1)} %bitcast.513, ...), custom_call_target="tpu_custom_call" | custom-call | tf_op jit(solution)/shard_map/attend/pallas_call | solution.py:225
  294.7 10.0 %collective-permute-start.13 = (bf16[256,768]{1,0:T(8,128)(2,1)}, bf16[256,768]{1,0:T(8,128)(2,1)}, u32[]{:S(2)}, u32[]{:S(2)}) collective-permute-start(bf16[256,768]{1,0:T(8,128)(2,1)} %get-tuple-element.160), channel_id=1, source_target_pairs={{0,24},{8,0},{16,8},{24,16},{1,25},{9,1},{17,9},{25,17},{2,26},{10... | collective-permute-start | bytes 1179656 | tf_op jit(solution)/shard_map/ppermute | solution.py:46
  305.5 17.2 %attend_back.2 = (f32[4,1,256,384]{3,2,1,0:T(8,128)}, f32[4,1,256,384]{3,2,1,0:T(8,128)}, bf16[4,1,256,384]{3,2,1,0:T(8,128)(2,1)}) custom-call(s32[1,32]{1,0:T(1,128)} %and_convert_fusion.need_ref, s32[12]{0:T(128)} %pad_add_fusion.1.base_ref, s32[1,4,1,256]{3,2,1,0:T(1,128)} %reshape.577.begin_ref, bf16[4,1,256,384]{3,2,1,0:T(8,128)(2,1)} %bitcast.514, ...), custom_call_target="tpu_custom_call" | custom-call | tf_op jit(solution)/shard_map/attend_back/pallas_call | solution.py:317
  326.7 34.0 %collective-permute-start.51 = (bf16[96,768]{1,0:T(8,128)(2,1)S(1)}, bf16[96,768]{1,0:T(8,128)(2,1)S(1)}, u32[]{:S(2)}, u32[]{:S(2)}) collective-permute-start(bf16[96,768]{1,0:T(8,128)(2,1)S(1)} %fusion.46), channel_id=1, source_target_pairs={{0,1},{1,0},{2,3},{3,2},{4,5},{5,4},{6,7},{7,6},{8,9},{9,8},{10,11... | collective-permute-start | bytes 442376 | tf_op jit(solution)/shard_map/ppermute | solution.py:74
  361.8 17.5 %collective-permute-done.51 = bf16[96,768]{1,0:T(8,128)(2,1)S(1)} collective-permute-done((bf16[96,768]{1,0:T(8,128)(2,1)S(1)}, bf16[96,768]{1,0:T(8,128)(2,1)S(1)}, u32[]{:S(2)}, u32[]{:S(2)}) %collective-permute-start.51) | collective-permute-done | bytes 147488 | tf_op jit(solution)/shard_map/ppermute | solution.py:74
  391.3 7.8 %exit_pass.2 = (bf16[4,256,768]{2,1,0:T(8,128)(2,1)}, bf16[4,256,768]{2,1,0:T(8,128)(2,1)}, f32[8,768]{1,0:T(8,128)}) custom-call(f32[4,256,384]{2,1,0:T(8,128)} %bitcast.549, f32[4,256,384]{2,1,0:T(8,128)} %bitcast.550, bf16[4,256,384]{2,1,0:T(8,128)(2,1)} %bitcast.565, f32[4,256,128]{2,1,0:T(8,128)} %bitcast.488, f32[4,256,128]{2,1,0:T(8,128)} %bitcast.496, ...), custom_call_target="tpu_custom_call" | custom-call | tf_op jit(solution)/shard_map/exit_pass/pallas_call | solution.py:421
  416.6 24.5 %collective-permute-done.19 = bf16[256,768]{1,0:T(8,128)(2,1)S(1)} collective-permute-done((bf16[256,768]{1,0:T(8,128)(2,1)}, bf16[256,768]{1,0:T(8,128)(2,1)S(1)}, u32[]{:S(2)}, u32[]{:S(2)}) %collective-permute-start.19) | collective-permute-done | bytes 393248 | tf_op jit(solution)/shard_map/ppermute | solution.py:46
  451.4 6.6 %collective-permute-done.23 = bf16[256,768]{1,0:T(8,128)(2,1)S(1)} collective-permute-done((bf16[256,768]{1,0:T(8,128)(2,1)S(1)}, bf16[256,768]{1,0:T(8,128)(2,1)S(1)}, u32[]{:S(2)}, u32[]{:S(2)}) %collective-permute-start.23) | collective-permute-done | bytes 393248 | tf_op jit(solution)/shard_map/ppermute | solution.py:38
  458.0 15.6 %collective-permute-done.22 = bf16[256,768]{1,0:T(8,128)(2,1)S(1)} collective-permute-done((bf16[256,768]{1,0:T(8,128)(2,1)S(1)}, bf16[256,768]{1,0:T(8,128)(2,1)S(1)}, u32[]{:S(2)}, u32[]{:S(2)}) %collective-permute-start.22) | collective-permute-done | bytes 393248 | tf_op jit(solution)/shard_map/ppermute | solution.py:38
  476.6 17.1 %attend_back.3 = (f32[4,1,256,384]{3,2,1,0:T(8,128)}, f32[4,1,256,384]{3,2,1,0:T(8,128)}, bf16[4,1,256,384]{3,2,1,0:T(8,128)(2,1)}) custom-call(s32[1,32]{1,0:T(1,128)} %and_convert_fusion.need_ref, s32[12]{0:T(128)} %pad_add_fusion.1.base_ref, s32[1,4,1,256]{3,2,1,0:T(1,128)} %reshape.577.begin_ref, bf16[4,1,256,384]{3,2,1,0:T(8,128)(2,1)} %bitcast.509, ...), custom_call_target="tpu_custom_call" | custom-call | tf_op jit(solution)/shard_map/attend_back/pallas_call | solution.py:317
  495.2 7.6 %feed_back.3 = (bf16[4,256,768]{2,1,0:T(8,128)(2,1)}, f32[4,256,768]{2,1,0:T(8,128)}, f32[8,768]{1,0:T(8,128)}) custom-call(bf16[4,256,768]{2,1,0:T(8,128)(2,1)} %copy-done.2, bf16[4,256,768]{2,1,0:T(8,128)(2,1)} %pad_maximum_fusion.x_ref.refs_4_, bf16[4,256,768]{2,1,0:T(8,128)(2,1)} %get-tuple-element.72.slope_ref, bf16[8,320,768]{2,1,0:T(8,128)(2,1)} %bitcast.468, ...), custom_call_target="tpu_custom_call" | custom-call | tf_op jit(solution)/shard_map/feed_back/pallas_call | solution.py:367
  512.4 17.0 %collective-permute-start.33 = (bf16[96,768]{1,0:T(8,128)(2,1)S(1)}, bf16[96,768]{1,0:T(8,128)(2,1)S(1)}, u32[]{:S(2)}, u32[]{:S(2)}) collective-permute-start(bf16[96,768]{1,0:T(8,128)(2,1)S(1)} %fusion.44), channel_id=1, source_target_pairs={{0,1},{1,0},{2,3},{3,2},{4,5},{5,4},{6,7},{7,6},{8,9},{9,8},{10,11... | collective-permute-start | bytes 442376 | tf_op jit(solution)/shard_map/ppermute | solution.py:74
  545.1 7.8 %exit_pass.3 = (bf16[4,256,768]{2,1,0:T(8,128)(2,1)}, bf16[4,256,768]{2,1,0:T(8,128)(2,1)}, f32[8,768]{1,0:T(8,128)}) custom-call(f32[4,256,384]{2,1,0:T(8,128)} %bitcast.547, f32[4,256,384]{2,1,0:T(8,128)} %bitcast.548, bf16[4,256,384]{2,1,0:T(8,128)(2,1)} %bitcast.93.refs_0_, f32[4,256,128]{2,1,0:T(8,128)} %bitcast.489, f32[4,256,128]{2,1,0:T(8,128)} %bitcast.497, ...), custom_call_target="tpu_custom_call" | custom-call | tf_op jit(solution)/shard_map/exit_pass/pallas_call | solution.py:421
  556.4 8.7 %collective-permute-start.54 = (f32[8,10,24]{2,0,1:T(8,128)S(1)}, f32[8,10,24]{2,0,1:T(8,128)S(1)}, u32[]{:S(2)}, u32[]{:S(2)}) collective-permute-start(f32[8,10,24]{2,0,1:T(8,128)S(1)} %get-tuple-element.186), channel_id=1, source_target_pairs={{0,24},{8,0},{16,8},{24,16},{1,25},{9,1},{17,9},{25,17},{2,26},{10... | collective-permute-start | bytes 23048 | tf_op jit(solution)/shard_map/ppermute | solution.py:630
  565.9 4.6 fusion.84
  570.7 3.9 collective-permute-start.27
  588.8 5.5 collective-permute-done.48
  599.9 4.3 collective-permute-done.42
  612.5 5.8 collective-permute-done.29
  (531 shorter events, 222.3 us)
Async XLA Ops:
  7.2 43.7 %all-gather.5.cloned.1.call-start = ((), (), s32[]{:S(2)}) async-start(), calls=%async_computation | async-start | bytes 4423680 | tf_op jit(solution)/shard_map/all_gather | solution.py:525
  12.4 76.6 %all-gather.7.cloned.1.call-start = ((), (), s32[]{:S(2)}) async-start(), calls=%async_computation.1 | async-start | bytes 4423680 | tf_op jit(solution)/shard_map/all_gather | solution.py:525
  18.6 29.0 %collective-permute-start.1 = (bf16[256,768]{1,0:T(8,128)(2,1)S(1)}, bf16[256,768]{1,0:T(8,128)(2,1)S(1)}, u32[]{:S(2)}, u32[]{:S(2)}) collective-permute-start(bf16[256,768]{1,0:T(8,128)(2,1)S(1)} %bitcast.500), channel_id=1, source_target_pairs={{0,16},{8,24},{16,0},{24,8},{1,17},{9,25},{17,1},{25,9},{2,18},{10... | collective-permute-start | bytes 1179656 | tf_op jit(solution)/shard_map/ppermute | solution.py:38
  21.2 26.4 %collective-permute-start = (bf16[256,768]{1,0:T(8,128)(2,1)S(1)}, bf16[256,768]{1,0:T(8,128)(2,1)}, u32[]{:S(2)}, u32[]{:S(2)}) collective-permute-start(bf16[256,768]{1,0:T(8,128)(2,1)S(1)} %bitcast.501), channel_id=1, source_target_pairs={{0,24},{8,0},{16,8},{24,16},{1,25},{9,1},{17,9},{25,17},{2,26},{10... | collective-permute-start | bytes 1179656 | tf_op jit(solution)/shard_map/ppermute | solution.py:38
  23.3 83.2 %collective-permute-start.16 = (bf16[256,768]{1,0:T(8,128)(2,1)}, bf16[256,768]{1,0:T(8,128)(2,1)S(1)}, u32[]{:S(2)}, u32[]{:S(2)}) collective-permute-start(bf16[256,768]{1,0:T(8,128)(2,1)} %get-tuple-element.166), channel_id=1, source_target_pairs={{0,8},{8,16},{16,24},{24,0},{1,9},{9,17},{17,25},{25,1},{2,10},{10... | collective-permute-start | bytes 1179656 | tf_op jit(solution)/shard_map/ppermute | solution.py:38
  24.0 82.5 %collective-permute-start.15 = (bf16[256,768]{1,0:T(8,128)(2,1)}, bf16[256,768]{1,0:T(8,128)(2,1)S(1)}, u32[]{:S(2)}, u32[]{:S(2)}) collective-permute-start(bf16[256,768]{1,0:T(8,128)(2,1)} %get-tuple-element.166), channel_id=1, source_target_pairs={{0,16},{8,24},{16,0},{24,8},{1,17},{9,25},{17,1},{25,9},{2,18},{10... | collective-permute-start | bytes 1179656 | tf_op jit(solution)/shard_map/ppermute | solution.py:38
  32.5 74.0 %collective-permute-start.14 = (bf16[256,768]{1,0:T(8,128)(2,1)}, bf16[256,768]{1,0:T(8,128)(2,1)S(1)}, u32[]{:S(2)}, u32[]{:S(2)}) collective-permute-start(bf16[256,768]{1,0:T(8,128)(2,1)} %get-tuple-element.166), channel_id=1, source_target_pairs={{0,24},{8,0},{16,8},{24,16},{1,25},{9,1},{17,9},{25,17},{2,26},{10... | collective-permute-start | bytes 1179656 | tf_op jit(solution)/shard_map/ppermute | solution.py:38
  101.1 27.9 %collective-permute-start.3 = (bf16[4,1,256,384]{3,2,1,0:T(8,128)(2,1)}, bf16[4,1,256,384]{3,2,1,0:T(8,128)(2,1)S(1)}, u32[]{:S(2)}, u32[]{:S(2)}) collective-permute-start(bf16[4,1,256,384]{3,2,1,0:T(8,128)(2,1)} %bitcast.510), channel_id=1, source_target_pairs={{0,1},{2,3},{4,5},{6,7},{8,9},{10,11},{12,13},{14,15},{16,17},{18,... | collective-permute-start | bytes 2359304 | tf_op jit(solution)/shard_map/ppermute | solution.py:556
  149.9 34.2 %collective-permute-start.5 = (bf16[256,768]{1,0:T(8,128)(2,1)}, bf16[256,768]{1,0:T(8,128)(2,1)}, u32[]{:S(2)}, u32[]{:S(2)}) collective-permute-start(bf16[256,768]{1,0:T(8,128)(2,1)} %get-tuple-element.164), channel_id=1, source_target_pairs={{0,16},{8,24},{16,0},{24,8},{1,17},{9,25},{17,1},{25,9},{2,18},{10... | collective-permute-start | bytes 1179656 | tf_op jit(solution)/shard_map/ppermute | solution.py:46
  149.9 34.2 %collective-permute-start.4 = (bf16[256,768]{1,0:T(8,128)(2,1)}, bf16[256,768]{1,0:T(8,128)(2,1)}, u32[]{:S(2)}, u32[]{:S(2)}) collective-permute-start(bf16[256,768]{1,0:T(8,128)(2,1)} %get-tuple-element.162), channel_id=1, source_target_pairs={{0,8},{8,16},{16,24},{24,0},{1,9},{9,17},{17,25},{25,1},{2,10},{10... | collective-permute-start | bytes 1179656 | tf_op jit(solution)/shard_map/ppermute | solution.py:46
  186.7 28.1 %collective-permute-start.8 = (bf16[256,768]{1,0:T(8,128)(2,1)S(1)}, bf16[256,768]{1,0:T(8,128)(2,1)S(1)}, u32[]{:S(2)}, u32[]{:S(2)}) collective-permute-start(bf16[256,768]{1,0:T(8,128)(2,1)S(1)} %get-tuple-element.148), channel_id=1, source_target_pairs={{0,16},{8,24},{16,0},{24,8},{1,17},{9,25},{17,1},{25,9},{2,18},{10... | collective-permute-start | bytes 1179656 | tf_op jit(solution)/shard_map/ppermute | solution.py:38
  188.7 26.1 %collective-permute-start.7 = (bf16[256,768]{1,0:T(8,128)(2,1)S(1)}, bf16[256,768]{1,0:T(8,128)(2,1)S(1)}, u32[]{:S(2)}, u32[]{:S(2)}) collective-permute-start(bf16[256,768]{1,0:T(8,128)(2,1)S(1)} %get-tuple-element.148), channel_id=1, source_target_pairs={{0,24},{8,0},{16,8},{24,16},{1,25},{9,1},{17,9},{25,17},{2,26},{10... | collective-permute-start | bytes 1179656 | tf_op jit(solution)/shard_map/ppermute | solution.py:38
  224.7 51.3 %collective-permute-start.10 = (bf16[4,1,256,384]{3,2,1,0:T(8,128)(2,1)}, bf16[4,1,256,384]{3,2,1,0:T(8,128)(2,1)S(1)}, u32[]{:S(2)}, u32[]{:S(2)}) collective-permute-start(bf16[4,1,256,384]{3,2,1,0:T(8,128)(2,1)} %bitcast.515), channel_id=1, source_target_pairs={{0,1},{2,3},{4,5},{6,7},{8,9},{10,11},{12,13},{14,15},{16,17},{18,... | collective-permute-start | bytes 2359304 | tf_op jit(solution)/shard_map/ppermute | solution.py:556
  272.2 51.0 %collective-permute-start.50 = (bf16[2,96,768]{2,1,0:T(8,128)(2,1)}, bf16[2,96,768]{2,1,0:T(8,128)(2,1)}, u32[]{:S(2)}, u32[]{:S(2)}) collective-permute-start(bf16[2,96,768]{2,1,0:T(8,128)(2,1)} %fusion.36), channel_id=1, source_target_pairs={{0,4},{2,6},{4,0},{6,2},{1,5},{3,7},{5,1},{7,3},{8,12},{10,14},{12... | collective-permute-start | bytes 884744 | tf_op jit(solution)/shard_map/ppermute | solution.py:74
  276.1 50.7 %collective-permute-start.44 = (bf16[2,104,768]{2,1,0:T(8,128)(2,1)}, bf16[2,104,768]{2,1,0:T(8,128)(2,1)}, u32[]{:S(2)}, u32[]{:S(2)}) collective-permute-start(bf16[2,104,768]{2,1,0:T(8,128)(2,1)} %fusion.32), channel_id=1, source_target_pairs={{0,1},{1,0},{2,3},{3,2},{4,5},{5,4},{6,7},{7,6},{8,9},{9,8},{10,11... | collective-permute-start | bytes 958472 | tf_op jit(solution)/shard_map/ppermute | solution.py:74
  294.7 91.1 %collective-permute-start.13 = (bf16[256,768]{1,0:T(8,128)(2,1)}, bf16[256,768]{1,0:T(8,128)(2,1)}, u32[]{:S(2)}, u32[]{:S(2)}) collective-permute-start(bf16[256,768]{1,0:T(8,128)(2,1)} %get-tuple-element.160), channel_id=1, source_target_pairs={{0,24},{8,0},{16,8},{24,16},{1,25},{9,1},{17,9},{25,17},{2,26},{10... | collective-permute-start | bytes 1179656 | tf_op jit(solution)/shard_map/ppermute | solution.py:46
  304.8 81.1 %collective-permute-start.12 = (bf16[256,768]{1,0:T(8,128)(2,1)}, bf16[256,768]{1,0:T(8,128)(2,1)}, u32[]{:S(2)}, u32[]{:S(2)}) collective-permute-start(bf16[256,768]{1,0:T(8,128)(2,1)} %get-tuple-element.161), channel_id=1, source_target_pairs={{0,16},{8,24},{16,0},{24,8},{1,17},{9,25},{17,1},{25,9},{2,18},{10... | collective-permute-start | bytes 1179656 | tf_op jit(solution)/shard_map/ppermute | solution.py:46
  304.8 81.1 %collective-permute-start.11 = (bf16[256,768]{1,0:T(8,128)(2,1)}, bf16[256,768]{1,0:T(8,128)(2,1)}, u32[]{:S(2)}, u32[]{:S(2)}) collective-permute-start(bf16[256,768]{1,0:T(8,128)(2,1)} %get-tuple-element.159), channel_id=1, source_target_pairs={{0,8},{8,16},{16,24},{24,0},{1,9},{9,17},{17,25},{25,1},{2,10},{10... | collective-permute-start | bytes 1179656 | tf_op jit(solution)/shard_map/ppermute | solution.py:46
  323.9 66.5 %collective-permute-start.17 = (bf16[4,1,256,384]{3,2,0,1:T(8,128)(2,1)S(1)}, bf16[4,1,256,384]{3,2,0,1:T(8,128)(2,1)S(1)}, u32[]{:S(2)}, u32[]{:S(2)}) collective-permute-start(bf16[4,1,256,384]{3,2,0,1:T(8,128)(2,1)S(1)} %bitcast.615), channel_id=1, source_target_pairs={{1,0},{3,2},{5,4},{7,6},{9,8},{11,10},{13,12},{15,14},{17,16},{19,... | collective-permute-start | bytes 2359304 | tf_op jit(solution)/shard_map/ppermute | solution.py:584
  326.7 52.5 %collective-permute-start.51 = (bf16[96,768]{1,0:T(8,128)(2,1)S(1)}, bf16[96,768]{1,0:T(8,128)(2,1)S(1)}, u32[]{:S(2)}, u32[]{:S(2)}) collective-permute-start(bf16[96,768]{1,0:T(8,128)(2,1)S(1)} %fusion.46), channel_id=1, source_target_pairs={{0,1},{1,0},{2,3},{3,2},{4,5},{5,4},{6,7},{7,6},{8,9},{9,8},{10,11... | collective-permute-start | bytes 442376 | tf_op jit(solution)/shard_map/ppermute | solution.py:74
  405.3 35.8 %collective-permute-start.19 = (bf16[256,768]{1,0:T(8,128)(2,1)}, bf16[256,768]{1,0:T(8,128)(2,1)S(1)}, u32[]{:S(2)}, u32[]{:S(2)}) collective-permute-start(bf16[256,768]{1,0:T(8,128)(2,1)} %get-tuple-element.158), channel_id=1, source_target_pairs={{0,16},{8,24},{16,0},{24,8},{1,17},{9,25},{17,1},{25,9},{2,18},{10... | collective-permute-start | bytes 1179656 | tf_op jit(solution)/shard_map/ppermute | solution.py:46
  406.1 35.0 %collective-permute-start.18 = (bf16[256,768]{1,0:T(8,128)(2,1)S(1)}, bf16[256,768]{1,0:T(8,128)(2,1)S(1)}, u32[]{:S(2)}, u32[]{:S(2)}) collective-permute-start(bf16[256,768]{1,0:T(8,128)(2,1)S(1)} %get-tuple-element.156), channel_id=1, source_target_pairs={{0,8},{8,16},{16,24},{24,0},{1,9},{9,17},{17,25},{25,1},{2,10},{10... | collective-permute-start | bytes 1179656 | tf_op jit(solution)/shard_map/ppermute | solution.py:46
  413.6 34.9 %collective-permute-start.31 = (bf16[2,2,96,768]{3,2,1,0:T(8,128)(2,1)}, bf16[2,2,96,768]{3,2,1,0:T(8,128)(2,1)}, u32[]{:S(2)}, u32[]{:S(2)}) collective-permute-start(bf16[2,2,96,768]{3,2,1,0:T(8,128)(2,1)} %fusion.28), channel_id=1, source_target_pairs={{0,2},{2,0},{4,6},{6,4},{1,3},{3,1},{5,7},{7,5},{8,10},{10,8},{12,... | collective-permute-start | bytes 1769480 | tf_op jit(solution)/shard_map/ppermute | solution.py:74
  444.1 29.5 %collective-permute-start.22 = (bf16[256,768]{1,0:T(8,128)(2,1)S(1)}, bf16[256,768]{1,0:T(8,128)(2,1)S(1)}, u32[]{:S(2)}, u32[]{:S(2)}) collective-permute-start(bf16[256,768]{1,0:T(8,128)(2,1)S(1)} %convert_element_type.428), channel_id=1, source_target_pairs={{0,16},{8,24},{16,0},{24,8},{1,17},{9,25},{17,1},{25,9},{2,18},{10... | collective-permute-start | bytes 1179656 | tf_op jit(solution)/shard_map/ppermute | solution.py:38
  445.7 27.9 %collective-permute-start.21 = (bf16[256,768]{1,0:T(8,128)(2,1)S(1)}, bf16[256,768]{1,0:T(8,128)(2,1)S(1)}, u32[]{:S(2)}, u32[]{:S(2)}) collective-permute-start(bf16[256,768]{1,0:T(8,128)(2,1)S(1)} %convert_element_type.428), channel_id=1, source_target_pairs={{0,24},{8,0},{16,8},{24,16},{1,25},{9,1},{17,9},{25,17},{2,26},{10... | collective-permute-start | bytes 1179656 | tf_op jit(solution)/shard_map/ppermute | solution.py:38
  449.8 62.5 %collective-permute-start.32 = (bf16[2,96,768]{2,1,0:T(8,128)(2,1)S(1)}, bf16[2,96,768]{2,1,0:T(8,128)(2,1)S(1)}, u32[]{:S(2)}, u32[]{:S(2)}) collective-permute-start(bf16[2,96,768]{2,1,0:T(8,128)(2,1)S(1)} %fusion.34), channel_id=1, source_target_pairs={{0,4},{2,6},{4,0},{6,2},{1,5},{3,7},{5,1},{7,3},{8,12},{10,14},{12... | collective-permute-start | bytes 884744 | tf_op jit(solution)/shard_map/ppermute | solution.py:74
  493.7 51.4 %collective-permute-start.24 = (bf16[4,1,256,384]{3,2,0,1:T(8,128)(2,1)}, bf16[4,1,256,384]{3,2,0,1:T(8,128)(2,1)}, u32[]{:S(2)}, u32[]{:S(2)}) collective-permute-start(bf16[4,1,256,384]{3,2,0,1:T(8,128)(2,1)} %bitcast.614), channel_id=1, source_target_pairs={{1,0},{3,2},{5,4},{7,6},{9,8},{11,10},{13,12},{15,14},{17,16},{19,... | collective-permute-start | bytes 2359304 | tf_op jit(solution)/shard_map/ppermute | solution.py:584
  508.1 33.2 %collective-permute-start.40 = (bf16[2,2,104,768]{3,2,0,1:T(8,128)(2,1)}, bf16[2,2,104,768]{3,2,0,1:T(8,128)(2,1)}, u32[]{:S(2)}, u32[]{:S(2)}) collective-permute-start(bf16[2,2,104,768]{3,2,0,1:T(8,128)(2,1)} %fusion.25), channel_id=1, source_target_pairs={{0,2},{2,0},{4,6},{6,4},{1,3},{3,1},{5,7},{7,5},{8,10},{10,8},{12,... | collective-permute-start | bytes 1916936 | tf_op jit(solution)/shard_map/ppermute | solution.py:74
  539.8 45.4 %collective-permute-start.47 = (bf16[2,96,768]{2,1,0:T(8,128)(2,1)S(1)}, bf16[2,96,768]{2,1,0:T(8,128)(2,1)}, u32[]{:S(2)}, u32[]{:S(2)}) collective-permute-start(bf16[2,96,768]{2,1,0:T(8,128)(2,1)S(1)} %fusion.35), channel_id=1, source_target_pairs={{0,4},{2,6},{4,0},{6,2},{1,5},{3,7},{5,1},{7,3},{8,12},{10,14},{12... | collective-permute-start | bytes 884744 | tf_op jit(solution)/shard_map/ppermute | solution.py:74
  543.4 43.2 %collective-permute-start.41 = (bf16[2,104,768]{2,1,0:T(8,128)(2,1)}, bf16[2,104,768]{2,1,0:T(8,128)(2,1)}, u32[]{:S(2)}, u32[]{:S(2)}) collective-permute-start(bf16[2,104,768]{2,1,0:T(8,128)(2,1)} %fusion.31), channel_id=1, source_target_pairs={{0,1},{1,0},{2,3},{3,2},{4,5},{5,4},{6,7},{7,6},{8,9},{9,8},{10,11... | collective-permute-start | bytes 958472 | tf_op jit(solution)/shard_map/ppermute | solution.py:74
  570.7 38.9 %collective-permute-start.27 = (bf16[256,768]{1,0:T(8,128)(2,1)}, bf16[256,768]{1,0:T(8,128)(2,1)}, u32[]{:S(2)}, u32[]{:S(2)}) collective-permute-start(bf16[256,768]{1,0:T(8,128)(2,1)} %get-tuple-element.154), channel_id=1, source_target_pairs={{0,24},{8,0},{16,8},{24,16},{1,25},{9,1},{17,9},{25,17},{2,26},{10... | collective-permute-start | bytes 1179656 | tf_op jit(solution)/shard_map/ppermute | solution.py:46
  574.5 35.0 %collective-permute-start.26 = (bf16[256,768]{1,0:T(8,128)(2,1)}, bf16[256,768]{1,0:T(8,128)(2,1)}, u32[]{:S(2)}, u32[]{:S(2)}) collective-permute-start(bf16[256,768]{1,0:T(8,128)(2,1)} %get-tuple-element.155), channel_id=1, source_target_pairs={{0,16},{8,24},{16,0},{24,8},{1,17},{9,25},{17,1},{25,9},{2,18},{10... | collective-permute-start | bytes 1179656 | tf_op jit(solution)/shard_map/ppermute | solution.py:46
  (111 other events, 1103.5 us)
Sparse Core Ops, SparseCore 0:
  12.5 38.3 all-gather.4
  53.3 35.6 all-gather.6
